TPU v7x, 128 devices: a whole 4x4x4 slice. The times are simulated.
128 devices in a mesh: grp: 16 (over x, z_hi, core), seq: 8 (over y, z_lo).
Axes of the slice: x: 4, y: 4, z: 4 (z_hi: 2, z_lo: 2; z = z_hi * 2 + z_lo), core: 2. Of those that a mesh axis runs over, the one named last changes fastest.
Arguments:
- lengths: int32 [32], replicated, may hold values from 64 to 2048, as said below
- group_of: int32 [32], replicated, may hold values from 0 to 15, as said below
- query_pre: bfloat16 [32768, 8192], P(('grp', 'seq')), may hold values from -170 to 170
- key_pre: bfloat16 [32768, 1024], P(('grp', 'seq')), may hold values from -7 to 7
- value_pre: bfloat16 [32768, 1024], P(('grp', 'seq')), may hold values from -4 to 4
- query_new: bfloat16 [32, 8192], P(None, 'seq'), may hold values from -170 to 170
- key_new: bfloat16 [32, 1024], P(None, 'seq'), may hold values from -4 to 4
- value_new: bfloat16 [32, 1024], P(None, 'seq'), may hold values from -4 to 4
- hidden_new: bfloat16 [32, 8192], P(None, 'grp'), may hold values from -3 to 3
- out_weight: bfloat16 [8192, 8192], P('seq', 'grp'), may hold values from -0.0625 to 0.0625
- norm_gain: bfloat16 [8192], P('grp'), may hold values from 0.099609375 to 1.8984375
- gate_weight: bfloat16 [8192, 16384], P('grp', 'seq'), may hold values from -0.0625 to 0.0625
- up_weight: bfloat16 [8192, 16384], P('grp', 'seq'), may hold values from -0.0625 to 0.0625
- down_weight: bfloat16 [16384, 8192], P('seq', 'grp'), may hold values from -0.046875 to 0.046875
Outputs:
- prefill_attention: bfloat16 [32768, 8192], P(('grp', 'seq'))
- decode_hidden: bfloat16 [32, 8192], P(None, ('grp', 'seq'))
Inputs may be any that keep to these rules, and one draw needn't show every extreme that they name: Two requests have length exactly 2048 and are alone in their groups; the others have lengths from 64 to 512; the lengths in one group sum to at most 2048. `group_of`: every group holds at least one request and at most three.
All inputs are finite; a program needn't handle non-finite values.
Results may differ from a plain program's by a relative error of at most 0.0095.
Values may be sent and summed in bfloat16 or wider, within the bound.
A program may use at most 320 MiB of HBM per device.

v0:
```python
import math

import jax
import jax.numpy as jnp
from jax import lax
from jax.sharding import PartitionSpec as P

D = 8192
H = 64
KVH = 8
HD = 128


NEGATIVE = -1e30


def request_starts(lengths, group_of):
    index = jnp.arange(lengths.shape[0], dtype=jnp.int32)
    same = group_of[None, :] == group_of[:, None]
    before = index[None, :] < index[:, None]
    return jnp.sum(jnp.where(same & before, lengths[None, :], 0), axis=1)


def slot_owner(group_idx, starts, lengths, group_of, count):
    slots = jnp.arange(count, dtype=jnp.int32)
    inside = (
        (group_of[None, :] == group_idx)
        & (slots[:, None] >= starts[None, :])
        & (slots[:, None] < (starts + lengths)[None, :])
    )
    labels = jnp.arange(lengths.shape[0], dtype=jnp.int32) + 1
    return jnp.sum(jnp.where(inside, labels[None, :], 0), axis=1) - 1


def block_scores(queries, keys, owner_rows, owner_cols, row_first):
    count_q = queries.shape[0]
    count_k = keys.shape[0]
    kv_heads = keys.shape[1] // HD
    grouped = queries.shape[1] // (HD * kv_heads)
    query_heads = queries.reshape(count_q, kv_heads, grouped, HD)
    key_heads = keys.reshape(count_k, kv_heads, HD)
    scores = jnp.einsum(
        "qkgd,tkd->kgqt", query_heads, key_heads, preferred_element_type=jnp.float32
    ) * (1.0 / math.sqrt(HD))
    rows = row_first + jnp.arange(count_q, dtype=jnp.int32)
    columns = jnp.arange(count_k, dtype=jnp.int32)
    allowed = (
        (owner_rows[:, None] == owner_cols[None, :])
        & (owner_rows[:, None] >= 0)
        & (columns[None, :] <= rows[:, None])
    )
    return (jnp.where(allowed[None, None], scores, NEGATIVE), allowed)


def online_step(carry, queries, keys, values, owner_rows, owner_cols, row_first):
    top, total, accum = carry
    count = keys.shape[0]
    kv_heads = keys.shape[1] // HD
    scores, allowed = block_scores(queries, keys, owner_rows, owner_cols, row_first)
    new_top = jnp.maximum(top, jnp.max(scores, axis=-1))
    weights = jnp.where(allowed[None, None], jnp.exp(scores - new_top[..., None]), 0.0)
    total = jnp.sum(weights, axis=-1)
    value_heads = values.reshape(count, kv_heads, HD)
    mixed = jnp.einsum(
        "kgqt,tkd->qkgd",
        weights.astype(jnp.bfloat16),
        value_heads,
        preferred_element_type=jnp.float32,
    )
    accum = mixed
    return (new_top, total, accum)


def empty_carry(rows, kv_heads, grouped):
    init_top = jnp.full((kv_heads, grouped, rows), NEGATIVE, jnp.float32)
    init_total = jnp.zeros((kv_heads, grouped, rows), jnp.float32)
    init_acc = jnp.zeros((rows, kv_heads, grouped, HD), jnp.float32)
    return (init_top, init_total, init_acc)


def finish(mixed, total, owner_rows):
    live = owner_rows >= 0
    denom = jnp.where(live[None, None, :], total, 1.0)
    result = mixed / jnp.transpose(denom, (2, 0, 1))[..., None]
    result = jnp.where(live[:, None, None, None], result, 0.0)
    return result.reshape(result.shape[0], -1).astype(jnp.bfloat16)


def decode_attend(query_new, key_new, value_new, cache_keys, cache_values, owners):
    requests = query_new.shape[0]
    kv_heads = cache_keys.shape[1] // HD
    grouped = query_new.shape[1] // (HD * kv_heads)
    query_heads = query_new.reshape(requests, kv_heads, grouped, HD)
    key_heads = cache_keys.reshape(cache_keys.shape[0], kv_heads, HD)
    value_heads = cache_values.reshape(cache_values.shape[0], kv_heads, HD)
    scale = 1.0 / math.sqrt(HD)
    scores = (
        jnp.einsum("rkgd,tkd->rkgt", query_heads, key_heads, preferred_element_type=jnp.float32)
        * scale
    )
    own = (
        jnp.einsum(
            "rkgd,rkd->rkg",
            query_heads,
            key_new.reshape(requests, kv_heads, HD),
            preferred_element_type=jnp.float32,
        )
        * scale
    )
    match = owners[None, :] == jnp.arange(requests, dtype=jnp.int32)[:, None]
    scores = jnp.where(match[:, None, None, :], scores, NEGATIVE)
    top = jnp.maximum(jnp.max(scores, axis=-1), own)
    weights = jnp.where(match[:, None, None, :], jnp.exp(scores - top[..., None]), 0.0)
    own_weight = jnp.exp(own - top)
    total = jnp.sum(weights, axis=-1) + own_weight
    mixed = jnp.einsum(
        "rkgt,tkd->rkgd",
        weights.astype(jnp.bfloat16),
        value_heads,
        preferred_element_type=jnp.float32,
    )
    own_value = value_new.reshape(requests, kv_heads, 1, HD).astype(jnp.float32)
    mixed = mixed + own_weight.astype(jnp.bfloat16).astype(jnp.float32)[..., None] * own_value
    return (mixed / total[..., None]).reshape(requests, -1).astype(jnp.bfloat16)


def shards(
    lengths,
    group_of,
    query_pre,
    key_pre,
    value_pre,
    query_new,
    key_new,
    value_new,
    hidden_new,
    out_weight,
    norm_gain,
    gate_weight,
    up_weight,
    down_weight,
):
    seq_count = lax.axis_size("seq")
    seq_index = lax.axis_index("seq")
    group_idx = lax.axis_index("grp")
    tokens_dev = query_pre.shape[0]
    group_slots = tokens_dev * seq_count
    starts = request_starts(lengths, group_of)
    owners = slot_owner(group_idx, starts, lengths, group_of, group_slots)
    cache_keys, cache_values = (
        lax.all_to_all(key_pre, "seq", split_axis=1, concat_axis=0, tiled=True),
        lax.all_to_all(value_pre, "seq", split_axis=1, concat_axis=0, tiled=True),
    )
    my_first = seq_index * tokens_dev
    my_last = my_first + tokens_dev - 1
    owner_rows = lax.dynamic_slice_in_dim(owners, my_first, tokens_dev, 0)
    any_live = jnp.any(owner_rows >= 0)
    grouped = H // KVH
    piece_keys = lax.all_gather(key_pre, "seq", axis=0, tiled=True)
    piece_values = lax.all_gather(value_pre, "seq", axis=0, tiled=True)
    needed = (jnp.int32(0) <= my_last) & any_live

    def attend(state):
        return online_step(state, query_pre, piece_keys, piece_values, owner_rows, owners, my_first)

    def keep(state):
        return state

    top, total, accum = lax.cond(needed, attend, keep, empty_carry(tokens_dev, KVH, grouped))
    prefill_attention = finish(accum, total, owner_rows)
    attended = decode_attend(query_new, key_new, value_new, cache_keys, cache_values, owners)
    mine = group_of == group_idx
    attended = jnp.where(mine[:, None], attended, jnp.zeros_like(attended))
    decode_att = lax.psum(attended, "grp").astype(jnp.float32).astype(jnp.bfloat16)
    proj_part = jnp.dot(decode_att, out_weight, preferred_element_type=jnp.float32)
    projected = lax.psum(proj_part, "seq")
    resid = hidden_new.astype(jnp.float32) + projected
    squares = lax.psum(jnp.sum(resid * resid, axis=-1), "grp")
    normed = (
        resid * lax.rsqrt(squares / D + 1e-05)[:, None] * norm_gain.astype(jnp.float32)[None, :]
    ).astype(jnp.bfloat16)
    gate_part = jnp.dot(normed, gate_weight, preferred_element_type=jnp.float32)
    upper_part = jnp.dot(normed, up_weight, preferred_element_type=jnp.float32)
    gate, upper = lax.psum((gate_part, upper_part), "grp")
    hidden = (jax.nn.silu(gate) * upper).astype(jnp.bfloat16)
    down_part = jnp.dot(hidden, down_weight, preferred_element_type=jnp.float32)
    down_share = lax.psum_scatter(down_part, "seq", scatter_dimension=1, tiled=True)
    width = down_share.shape[1]
    resid_share = lax.dynamic_slice_in_dim(resid, seq_index * width, width, 1)
    decode_hidden = (resid_share + down_share).astype(jnp.bfloat16)
    return (prefill_attention, decode_hidden)


def solution(mesh):
    return jax.shard_map(
        shards,
        mesh=mesh,
        in_specs=(
            P(),
            P(),
            P(("grp", "seq"), None),
            P(("grp", "seq"), None),
            P(("grp", "seq"), None),
            P(None, "seq"),
            P(None, "seq"),
            P(None, "seq"),
            P(None, "grp"),
            P("seq", "grp"),
            P("grp"),
            P("grp", "seq"),
            P("grp", "seq"),
            P("seq", "grp"),
        ),
        out_specs=(P(("grp", "seq"), None), P(None, ("grp", "seq"))),
        check_vma=False,
    )
```

profile of v0, /device:TPU:1, one launch (start us, length us, event | category | flops | bytes accessed | tf_op | source)
XLA Modules:
  0.0 828.6 jit_solution(12726307764702582196)
XLA Ops:
  9.3 6.4 all-to-all-start
  24.4 3.7 all-to-all-start.1
  30.5 5.6 all-to-all-done.1
  36.1 2.1 fusion.25
  39.0 127.9 %all-reduce.5.cloned.1.call-done = bf16[32,1024]{1,0:T(8,128)(2,1)} async-done(((bf16[32,1024]{1,0:T(8,128)(2,1)}), bf16[32,1024]{1,0:T(8,128)(2,1)}) %all-reduce.5.cloned.1.call-update) | async-done | bytes 65552 | tf_op jit(solution)/shard_map/psum | solution.py:174
  166.9 2.2 fusion.47
  169.2 67.9 %all-reduce.7.cloned.1.call-done = f32[32,512]{1,0:T(8,128)} async-done(((f32[32,512]{1,0:T(8,128)}), f32[32,512]{1,0:T(8,128)}) %all-reduce.7.cloned.1.call-update) | async-done | bytes 65552 | tf_op jit(solution)/shard_map/psum | solution.py:176
  238.0 38.4 %psum.37 = f32[32]{0:T(128)S(1)} all-reduce(f32[32]{0:T(128)S(1)} %get-tuple-element.28), channel_id=1, replica_groups=mesh['grp'=16,'seq'=8] {'grp'}, use_global_device_ids=true, to_apply=%region_12.13 | all-reduce | flops 32 | bytes 256 | tf_op jit(solution)/shard_map/psum | solution.py:178
  277.6 2.8 fusion.43
  280.5 133.3 %all-reduce.9.cloned.1.call-done = (f32[32,2048]{1,0:T(8,128)}, f32[32,2048]{1,0:T(8,128)}) async-done(((f32[32,2048]{1,0:T(8,128)}, f32[32,2048]{1,0:T(8,128)}), (f32[32,2048]{1,0:T(8,128)}, f32[32,2048]{1,0:T(8,128)})) %all-reduce.9.cloned.1.call-update) | async-done | bytes 524304 | tf_op jit(solution)/shard_map/psum | solution.py:184
  413.8 3.4 convolution_bitcast_fusion
  420.3 30.3 %reduce-scatter.4.cloned.1.call-done = f32[64,32]{1,0:T(8,128)} async-done(((f32[512,32]{1,0:T(8,128)}), f32[64,32]{1,0:T(8,128)}) %reduce-scatter.4.cloned.1.call-update) | async-done | bytes 8208
  452.2 93.4 %all-gather.3.cloned.1.call-done = bf16[2048,1024]{1,0:T(8,128)(2,1)} async-done(((bf16[256,1024]{1,0:T(8,128)(2,1)}), bf16[2048,1024]{1,0:T(8,128)(2,1)}) %all-gather.3.cloned.1.call-update) | async-done | bytes 4194320 | tf_op jit(solution)/shard_map/all_gather | solution.py:159
  545.5 93.8 %all-gather.5.cloned.1.call-done = bf16[2048,1024]{1,0:T(8,128)(2,1)} async-done(((bf16[256,1024]{1,0:T(8,128)(2,1)}), bf16[2048,1024]{1,0:T(8,128)(2,1)}) %all-gather.5.cloned.1.call-update) | async-done | bytes 4194320 | tf_op jit(solution)/shard_map/all_gather | solution.py:160
  639.4 163.3 %conditional.1 = (f32[8,8,256]{2,1,0:T(8,128)}, f32[256,8,8,128]{3,0,2,1:T(8,128)}) conditional(s32[]{:T(128)} %convert_element_type.50, () %tuple.16, (s32[256]{0:T(256)S(1)}, s32[2048]{0:T(1024)S(1)}, s32[]{:T(128)}, bf16[2048,1024]{1,0:T(8,128)(2,1)}, bf16[256,8192]{1,0:T(8,128)(2,1)}, /*index=5*/bf16[2048,1024]{1,0:T(8,128)(2,1)}) %tuple.17), branch_computations={%region_3.4_spmd, %region_4.7_spmd} | conditional | flops 17618157568 | bytes 468070976 | solution.py:169
  640.1 5.4 copy.67
  645.5 3.2 copy.68
  648.7 52.7 %fusion = (f32[8,8,256]{2,1,0:T(8,128)S(1)}, f32[8,2048,256,8]{2,1,3,0:T(8,128)}) fusion(pred[256,2048]{0,1:T(8,128)(4,1)S(1)} %fusion.15, bf16[256,8,8,128]{3,2,1,0:T(8,128)(2,1)} %bitcast.116, bf16[2048,8,128,1]{2,1,0,3:T(8,128)(2,1)} %bitcast.117), kind=kOutput, calls=%fused_computation.2 | convolution fusion | flops 8690581504 | bytes 143196160 | tf_op jit(solution)/shard_map/cond/branch_1_fun/qkgd,tkd->kgqt/dot_general | solution.py:42
  701.4 5.3 copy.69
  706.7 54.0 %fusion.10 = f32[256,8,8,128]{3,0,2,1:T(8,128)} fusion(bf16[2048,8,128,1]{2,1,0,3:T(8,128)(2,1)} %bitcast.123, f32[8,2048,256,8]{2,1,3,0:T(8,128)} %get-tuple-element.34, f32[8,8,256]{2,1,0:T(8,128)S(1)} %broadcast_maximum_fusion, pred[256,2048]{0,1:T(8,128)(4,1)S(1)} %fusion.15), kind=kOutput, calls=%fused_computation.11 | convolution fusion | flops 8757706752 | bytes 147390464 | tf_op jit(solution)/shard_map/cond/branch_1_fun/kgqt,tkd->qkgd/dot_general | solution.py:64
  760.7 41.9 %fusion.2 = f32[8,8,256]{2,1,0:T(8,128)} fusion(f32[8,2048,256,8]{2,1,3,0:T(8,128)} %get-tuple-element.34, f32[8,8,256]{2,1,0:T(8,128)S(1)} %broadcast_maximum_fusion, pred[256,2048]{0,1:T(8,128)(4,1)S(1)} %fusion.15), kind=kLoop, calls=%fused_computation.4 | loop fusion | flops 167755776 | bytes 134873088 | tf_op jit(solution)/shard_map/cond/branch_1_fun/reduce_sum | solution.py:62
  803.5 5.4 select_convert_fusion
  808.9 2.7 copy.51
  811.6 10.2 %copy.100 = bf16[32,8,64,128]{3,1,2,0:T(8,128)(2,1)} copy(bf16[32,8,64,128]{3,2,1,0:T(8,128)(2,1)S(1)} %bitcast.118) | data formatting | bytes 8388608
  (58 shorter events, 21.7 us)
Async XLA Ops:
  7.2 269.2 %copy-start = (bf16[512,2048]{1,0:T(8,128)(2,1)S(1)}, bf16[512,2048]{1,0:T(8,128)(2,1)}, u32[]{:S(2)}) copy-start(bf16[512,2048]{1,0:T(8,128)(2,1)} %param.27) | copy-start | bytes 6291460
  7.2 20.9 %copy-start.3 = (bf16[32,1024]{1,0:T(8,128)(2,1)S(1)}, bf16[32,1024]{1,0:T(8,128)(2,1)}, u32[]{:S(2)}) copy-start(bf16[32,1024]{1,0:T(8,128)(2,1)} %param.21) | copy-start | bytes 196612
  9.3 15.1 %all-to-all-start = ((bf16[256,8,128]{2,0,1:T(8,128)(2,1)}), bf16[256,8,128]{2,0,1:T(8,128)(2,1)S(1)}, u32[]{:S(2)}, u32[]{:S(2)}) async-start(bf16[256,8,128]{2,0,1:T(8,128)(2,1)} %copy_bitcast_fusion.2), calls=%async_computation | async-start | bytes 1048576 | tf_op jit(solution)/shard_map/all_to_all | solution.py:151
  24.4 11.8 %all-to-all-start.1 = ((bf16[256,8,128]{2,0,1:T(8,128)(2,1)}), bf16[256,8,128]{2,0,1:T(8,128)(2,1)S(1)}, u32[]{:S(2)}, u32[]{:S(2)}) async-start(bf16[256,8,128]{2,0,1:T(8,128)(2,1)} %copy_bitcast_fusion.1), calls=%async_computation.1 | async-start | bytes 1048576 | tf_op jit(solution)/shard_map/all_to_all | solution.py:152
  28.1 138.8 %all-reduce.5.cloned.1.call-start = ((), (), s32[]{:S(2)}) async-start(), calls=%async_computation.5 | async-start | bytes 131072 | tf_op jit(solution)/shard_map/psum | solution.py:174
  28.7 1.3 copy-start.1
  28.7 140.5 %copy-start.6 = (bf16[512]{0:T(512)(128)(2,1)S(1)}, bf16[512]{0:T(512)(128)(2,1)}, u32[]{:S(2)}) copy-start(bf16[512]{0:T(512)(128)(2,1)} %param.26) | copy-start | bytes 3076
  28.7 208.4 %copy-start.4 = (bf16[32,512]{1,0:T(8,128)(2,1)S(1)}, bf16[32,512]{1,0:T(8,128)(2,1)}, u32[]{:S(2)}) copy-start(bf16[32,512]{1,0:T(8,128)(2,1)} %param.24) | copy-start | bytes 98308
  39.0 198.1 %all-reduce.7.cloned.1.call-start = ((), (), s32[]{:S(2)}) async-start(), calls=%async_computation.6 | async-start | bytes 131072 | tf_op jit(solution)/shard_map/psum | solution.py:176
  169.1 244.7 %all-reduce.9.cloned.1.call-start = ((), (), s32[]{:S(2)}) async-start(), calls=%async_computation.8 | async-start | bytes 1048576 | tf_op jit(solution)/shard_map/psum | solution.py:184
  280.5 170.2 %reduce-scatter.4.cloned.1.call-start = ((), (), s32[]{:S(2)}) async-start(), calls=%async_computation.7 | async-start | bytes 294912
  417.3 128.3 %all-gather.3.cloned.1.call-start = ((), (), s32[]{:S(2)}) async-start(), calls=%async_computation.3 | async-start | bytes 4718592 | tf_op jit(solution)/shard_map/all_gather | solution.py:159
  417.9 221.5 %all-gather.5.cloned.1.call-start = ((), (), s32[]{:S(2)}) async-start(), calls=%async_computation.4 | async-start | bytes 4718592 | tf_op jit(solution)/shard_map/all_gather | solution.py:160
  639.3 163.3 %copy-start.5 = (pred[256]{0:T(512)(128)(4,1)S(1)}, pred[256]{0:T(512)(128)(4,1)}, u32[]{:S(2)}) copy-start(pred[256]{0:T(512)(128)(4,1)} %get-tuple-element.31) | copy-start | bytes 772
  640.1 5.4 copy-start.2
Sparse Core Ops, SparseCore 0:
  39.1 127.7 all-reduce.4
  170.1 66.9 all-reduce.6
  280.6 133.2 all-reduce.8
  417.4 33.2 reduce-scatter.3
  452.2 93.3 all-gather.2
  547.0 92.2 all-gather.4
where the time goes:
time: 830 us; the launch traced here: 829 us
  waiting for transfers between devices  555 us (67%)
  matrix products  120 us (14%)
  other arithmetic  56.1 us (7%)
  blocking collectives  38.4 us (5%)
  local copies, waits for them, and re-layouts  33.9 us (4%)
  between operations  14.9 us (2%)
  starting transfers between devices  10.3 us (1%)
    psum x1, waiting for transfers between devices, shards(): gate, upper = lax.psum((gate_part, upper_part), 'grp')  133 us
    psum x1, waiting for transfers between devices, shards(): lax.psum(attended, 'grp').astype(jnp.float32).astype(jnp.bfloat16)  128 us
    all_gather x1, waiting for transfers between devices, shards(): piece_values = lax.all_gather(value_pre, 'seq', axis=0, tiled=True)  93.8 us
    all_gather x1, waiting for transfers between devices, shards(): piece_keys = lax.all_gather(key_pre, 'seq', axis=0, tiled=True)  93.4 us
    psum x1, waiting for transfers between devices, shards(): projected = lax.psum(proj_part, 'seq')  67.9 us
    dot_general x1, matrix products, online_step(): jnp.einsum('kgqt,tkd->qkgd', weights.astype(jnp.bfloat16), value_heads, p...  54 us
    dot_general x1, matrix products, block_scores(): jnp.einsum('qkgd,tkd->kgqt', query_heads, key_heads, preferred_element_ty...  52.7 us
    reduce_sum x1, other arithmetic, online_step(): total = jnp.sum(weights, axis=-1)  41.9 us
  transfers between devices with their start and end apart: 8, of which 8 were waited for; matrix products, arithmetic and copies ran while one was open for 1% of the time, Pallas kernels for 0%

commit v1 on v0

v1 whole, which is shorter than its diff:
```python
import functools
import math

import jax
import jax.numpy as jnp
from jax import lax
from jax.experimental import pallas as pl
from jax.experimental.pallas import tpu as pltpu
from jax.sharding import PartitionSpec as P

HD = 128
SEQ = 8
GRP = 16
ROWS = 256
KVH = 8
GROUPED = 8
REQS = 32
D = 8192
SCALE = 1.0 / math.sqrt(HD)
LOG2E = math.log2(math.e)
NEGATIVE = -1e30
FAR = -float(2**23)
F32 = jnp.float32
BF16 = jnp.bfloat16
NT = (((1,), (1,)), ((), ()))


def iota(shape, dim):
    return lax.broadcasted_iota(jnp.int32, shape, dim)


def as_column(row, count):
    eye = iota((count, 128), 0) == iota((count, 128), 1)
    return jnp.sum(jnp.where(eye, row, 0), axis=1, keepdims=True)


def request_tables(meta_ref):
    lengths = meta_ref[0:1, :]
    groups = meta_ref[1:2, :]
    len_col = as_column(lengths, 128)
    grp_col = as_column(groups, 128)
    before = (grp_col == groups) & (iota((128, 128), 0) < iota((128, 128), 1))
    starts = jnp.sum(jnp.where(before, len_col, 0), axis=0, keepdims=True)
    ranks = jnp.sum(jnp.where(before, 1, 0), axis=0, keepdims=True)
    return lengths, groups, starts, ranks


def owner_onehot(tables, group, first, count):
    lengths, groups, starts, _ = tables
    slot = first + iota((count, 128), 0)
    return (groups == group) & (slot >= starts) & (slot < starts + lengths)


def attend_kernel(meta_ref, q_ref, kv_ref, o_ref, qx, kx, top, total, accum, low):
    head = pl.program_id(0)
    seq = lax.axis_index("seq")
    group = lax.axis_index("grp")

    @pl.when(head == 0)
    def _():
        tables = request_tables(meta_ref)
        lengths, groups, starts, _ = tables
        lane = iota((ROWS, 128), 1)
        rows_in = owner_onehot(tables, group, seq * ROWS, ROWS)
        qx[...] = jnp.where(((lane < REQS) & ~rows_in) | (lane == 127), FAR, 0.0).astype(BF16)
        for part in range(SEQ):
            cols_in = owner_onehot(tables, group, part * ROWS, ROWS)
            none = jnp.sum(jnp.where(cols_in, 1.0, 0.0), axis=1, keepdims=True) == 0.0
            kx[part * ROWS : (part + 1) * ROWS, :] = jnp.where(cols_in | (none & (lane == 127)), 1.0, 0.0).astype(BF16)
        first = seq * ROWS
        touches = (groups == group) & (starts < first + ROWS) & (starts + lengths > first)
        low[0] = jnp.min(jnp.where(touches, starts, 4096))

    for a in range(GROUPED):
        top[a] = jnp.full((ROWS, 128), NEGATIVE, F32)
        total[a] = jnp.zeros((ROWS, 128), F32)
        accum[a] = jnp.zeros((ROWS, 128), F32)

    def block(j, diagonal):
        keys = kv_ref[pl.ds(2 * j, 2), 0, 0].reshape(512, HD)
        values = kv_ref[pl.ds(2 * j, 2), 0, 1].reshape(512, HD)
        keys = jnp.concatenate([keys, kx[pl.ds(pl.multiple_of(j * 512, 512), 512), :]], 1)
        if diagonal:
            causal = (j * 512 + iota((ROWS, 512), 1)) <= (seq * ROWS + iota((ROWS, 512), 0))
        scores = []
        for a in range(GROUPED):
            queries = jnp.concatenate([q_ref[:, a * HD : (a + 1) * HD], qx[...]], 1)
            scores.append(lax.dot_general(queries, keys, NT, preferred_element_type=F32))
        for a in range(GROUPED):
            s = scores[a]
            if diagonal:
                s = jnp.where(causal, s, NEGATIVE)
            old = top[a]
            m = s[:, 0:128]
            for i in range(1, 4):
                m = jnp.maximum(m, s[:, i * 128 : (i + 1) * 128])
            new = jnp.maximum(old, jnp.max(m, axis=1, keepdims=True))
            decay = jnp.exp2((old - new) * (SCALE * LOG2E))
            shift = new * (SCALE * LOG2E)
            p = jnp.concatenate(
                [jnp.exp2(s[:, i * 128 : (i + 1) * 128] * (SCALE * LOG2E) - shift) for i in range(4)], 1
            )
            t = p[:, 0:128]
            for i in range(1, 4):
                t = t + p[:, i * 128 : (i + 1) * 128]
            total[a] = total[a] * decay + t
            top[a] = new
            accum[a] = accum[a] * decay + jnp.dot(p.astype(BF16), values, preferred_element_type=F32)

    last = seq // 2
    begin = low[0] // 512

    @pl.when(begin <= last)
    def _():
        def step(j, carry):
            block(j, False)
            return carry

        lax.fori_loop(begin, last, step, 0)
        block(last, True)

    live = jnp.min(qx[...].astype(F32)[:, 0:128] * jnp.where(iota((ROWS, 128), 1) < REQS, 1.0, 0.0), axis=1, keepdims=True)
    held = jnp.sum(jnp.where((iota((ROWS, 128), 1) < REQS) & (qx[...].astype(F32) == 0.0), 1.0, 0.0), axis=1, keepdims=True)
    del live
    for a in range(GROUPED):
        t = jnp.sum(total[a], axis=1, keepdims=True)
        out = jnp.where(held > 0.0, accum[a] / jnp.where(held > 0.0, t, 1.0), 0.0)
        o_ref[:, a * HD : (a + 1) * HD] = out.astype(BF16)


def attend(meta, queries, kvg):
    return pl.pallas_call(
        attend_kernel,
        grid=(KVH,),
        out_shape=jax.ShapeDtypeStruct((ROWS, D), BF16),
        in_specs=[
            pl.BlockSpec((8, 128), lambda h: (0, 0)),
            pl.BlockSpec((ROWS, GROUPED * HD), lambda h: (0, h)),
            pl.BlockSpec((SEQ, 1, 2, ROWS, HD), lambda h: (0, h, 0, 0, 0)),
        ],
        out_specs=pl.BlockSpec((ROWS, GROUPED * HD), lambda h: (0, h)),
        scratch_shapes=[
            pltpu.VMEM((ROWS, 128), BF16),
            pltpu.VMEM((SEQ * ROWS, 128), BF16),
            pltpu.VMEM((GROUPED, ROWS, 128), F32),
            pltpu.VMEM((GROUPED, ROWS, 128), F32),
            pltpu.VMEM((GROUPED, ROWS, 128), F32),
            pltpu.SMEM((1,), jnp.int32),
        ],
        compiler_params=pltpu.CompilerParams(vmem_limit_bytes=50 << 20),
        cost_estimate=pl.CostEstimate(flops=17 << 30, bytes_accessed=16 << 20, transcendentals=32 << 20),
        name="attend",
    )(meta, queries, kvg)


def remote(src, dst, send_sem, recv_sem, device):
    return pltpu.make_async_remote_copy(src_ref=src, dst_ref=dst, send_sem=send_sem, recv_sem=recv_sem, device_id=device)


class Exchange:
    def __init__(self, axis, count, me, source, landing, send_sem, recv_sem, spread=lambda i: i):
        self.axis, self.count, self.me, self.spread = axis, count, me, spread
        self.source, self.landing, self.send_sem, self.recv_sem = source, landing, send_sem, recv_sem

    def start(self):
        for i in range(1, self.count):
            peer = (self.me + i) % self.count
            remote(
                self.source(peer),
                self.landing.at[self.me],
                self.send_sem.at[i],
                self.recv_sem.at[self.me],
                {self.axis: self.spread(peer)},
            ).start()

    def wait(self):
        for i in range(1, self.count):
            peer = (self.me + i) % self.count
            copy = remote(
                self.source(peer),
                self.landing.at[peer],
                self.send_sem.at[i],
                self.recv_sem.at[peer],
                {self.axis: self.spread(peer)},
            )
            copy.wait_send()
            copy.wait_recv()


def step_kernel(
    meta_ref, k_ref, v_ref, qn_ref, kn_ref, vn_ref, hid_ref, gain_ref, ow_ref, gw_ref, uw_ref, dw_ref,
    kvg, dec_ref,
    owb, gwb, uwb, dwb, qmsg, qall, pmsg, part, amsg, aall, pblk, prs, rmsg, rall, gmsg, grs, hmsg, hall, dblk, drs,
    wsem, lsem, kss, krs, qss, qrs, pss, prsem, ass, ars, oss, ors, rss, rrs, gss, grsem, hss, hrs, dss, drsem,
):
    seq = lax.axis_index("seq")
    group = lax.axis_index("grp")
    y, z = seq // 2, seq % 2
    pair = seq + 1 - 2 * z
    up, down = (seq + 2) % SEQ, (seq + 6) % SEQ

    barrier = pltpu.get_barrier_semaphore()
    for i in range(1, SEQ):
        pl.semaphore_signal(barrier, inc=1, device_id={"seq": (seq + i) % SEQ})
    for i in range(1, GRP):
        pl.semaphore_signal(barrier, inc=1, device_id={"grp": (group + i) % GRP})

    def own_copy(h, which):
        src = (k_ref, v_ref)[which].at[:, pl.ds(pl.multiple_of(h * HD, HD), HD)]
        return pltpu.make_async_copy(src, kvg.at[seq, h, which], lsem.at[h, which])

    def own_start(h, carry):
        own_copy(h, 0).start()
        own_copy(h, 1).start()
        return carry

    lax.fori_loop(0, KVH, own_start, 0)
    weights = [(ow_ref, owb), (gw_ref, gwb), (uw_ref, uwb), (dw_ref, dwb)]
    for i, (src, dst) in enumerate(weights):
        pltpu.make_async_copy(src, dst, wsem.at[i]).start()

    def weight_wait(i):
        pltpu.make_async_copy(weights[i][0], weights[i][1], wsem.at[i]).wait()

    lengths, groups, starts, ranks = request_tables(meta_ref)
    slot32 = iota((REQS, 128), 0) % 4
    pick = (groups == group) & (ranks == slot32)
    pick32 = jnp.where(pick, 1.0, 0.0).astype(BF16)[:, 0:REQS]
    block32 = iota((REQS, HD), 0) // 4
    spread_q = jnp.dot(pick32, qn_ref[...], preferred_element_type=F32)
    mine_q = jnp.zeros((REQS, HD), F32)
    for a in range(GROUPED):
        mine_q = mine_q + jnp.where(block32 == a, spread_q[:, a * HD : (a + 1) * HD], 0.0)
    qmsg[...] = mine_q.astype(BF16)
    qall[seq] = mine_q.astype(BF16)

    pl.semaphore_wait(barrier, SEQ + GRP - 2)

    ex_q = Exchange("seq", SEQ, seq, lambda p: qmsg, qall, qss, qrs)
    ex_p = Exchange("seq", SEQ, seq, lambda p: pmsg.at[p], part, pss, prsem)
    ex_a = Exchange("grp", GRP, group, lambda p: amsg, aall, ass, ars)
    ex_o = Exchange("seq", SEQ, seq, lambda p: pblk.at[p // 2], prs, oss, ors)
    ex_r = Exchange("seq", 4, y, lambda p: rmsg, rall, rss, rrs, lambda p: 2 * p + z)
    ex_g = Exchange("grp", GRP, group, lambda p: gmsg.at[p], grs, gss, grsem)
    ex_h = Exchange("grp", GRP, group, lambda p: hmsg, hall, hss, hrs)
    ex_d = Exchange("seq", SEQ, seq, lambda p: dblk.at[p // 2], drs, dss, drsem)

    def relay(h, slot, shard, dst):
        return remote(kvg.at[shard, h], kvg.at[shard, h], kss.at[h, slot], krs.at[shard, h], {"seq": dst})

    turn = ((y + 1) // 2 + 1) % 2
    cross = 2 * (1 - y % 2) + z
    far = (seq + 4) % SEQ

    def sends(h):
        return [
            (0, seq, pair, y >= 0),
            (1, seq, up, y < 3),
            (2, seq, down, (y == 0) | ((y == 1) & (h % 2 == 1))),
            (3, pair, up, y < 3),
            (4, pair, down, y == 0),
            (5, cross, (seq + 2 + 4 * turn) % SEQ, h % 2 == turn),
            (6, far, pair, y >= 2),
        ]

    def start(h, slots):
        for slot, shard, dst, on in sends(h):
            if slot in slots:

                @pl.when(on)
                def _():
                    relay(h, slot, shard, dst).start()

    def arrived(h, shard):
        relay(h, 0, shard, pair).wait_recv()

    def relay_first(h):
        own_copy(h, 0).wait()
        own_copy(h, 1).wait()
        start(h, (0, 1, 2))

    def relay_second(h):
        arrived(h, pair)
        start(h, (3, 4))

        @pl.when(h % 2 == turn)
        def _():
            arrived(h, cross)

        start(h, (5,))

    def relay_third(h):
        @pl.when(y >= 2)
        def _():
            arrived(h, far)

        start(h, (6,))

    def relay_last(h):
        for t in range(SEQ):
            seen = ((t == cross) & (h % 2 == turn)) | ((t == far) & (y >= 2))

            @pl.when((t // 2 < y) & jnp.logical_not(seen))
            def _():
                arrived(h, t)

    def relay_sent(h):
        for slot, shard, dst, on in sends(h):

            @pl.when(on)
            def _():
                relay(h, slot, shard, dst).wait_send()

    def dec0():
        ex_q.start()

    def dec1():
        ex_q.wait()
        start_c = jnp.sum(jnp.where(pick, starts, 0), axis=1, keepdims=True)
        len_c = jnp.sum(jnp.where(pick, lengths, 0), axis=1, keepdims=True)
        pos = seq * ROWS + iota((REQS, ROWS), 1)
        allowed = (pos >= start_c) & (pos < start_c + len_c)
        for t in range(SEQ):
            s = lax.dot_general(qall[t], k_ref[:, t * HD : (t + 1) * HD], NT, preferred_element_type=F32) * SCALE
            s = jnp.where(allowed, s, NEGATIVE)
            m = jnp.max(s, axis=1, keepdims=True)
            p = jnp.where(allowed, jnp.exp(s - m), 0.0)
            l = jnp.sum(p, axis=1, keepdims=True)
            pmsg[t, 0] = jnp.dot(p.astype(BF16), v_ref[:, t * HD : (t + 1) * HD], preferred_element_type=F32)
            pmsg[t, 1] = jnp.where(iota((REQS, HD), 1) == 0, m, l)
        part[seq] = pmsg[seq]
        ex_p.start()

    def dec2():
        ex_p.wait()
        key_row = jnp.dot(pick32, kn_ref[...], preferred_element_type=F32)
        value_row = jnp.dot(pick32, vn_ref[...], preferred_element_type=F32)
        own = jnp.sum(qmsg[...].astype(F32) * key_row, axis=1, keepdims=True) * SCALE
        top = own
        for t in range(SEQ):
            top = jnp.maximum(top, part[t, 1][:, 0:1])
        weight = jnp.exp(own - top)
        total = weight
        mixed = weight.astype(BF16).astype(F32) * value_row
        for t in range(SEQ):
            scale = jnp.exp(part[t, 1][:, 0:1] - top)
            total = total + scale * part[t, 1][:, 1:2]
            mixed = mixed + scale * part[t, 0]
        out = (mixed / total).astype(BF16)
        amsg[...] = out
        aall[group] = out
        ex_a.start()

    def dec3():
        ex_a.wait()
        rank_col = as_column(ranks, REQS)
        grp_col = as_column(groups, REQS)
        target = jnp.concatenate([grp_col * 32 + a * 4 + rank_col for a in range(GROUPED)], 0)
        gather = jnp.where(iota((256, 512), 1) == target, 1.0, 0.0).astype(BF16)
        rows = jnp.dot(gather, aall[...].reshape(512, HD), preferred_element_type=F32).astype(BF16)
        att = jnp.concatenate([rows[a * 32 : (a + 1) * 32] for a in range(GROUPED)], 1)
        weight_wait(0)
        proj = jnp.dot(att, owb[...], preferred_element_type=F32)
        for b in range(4):
            pblk[b] = proj[:, b * 128 : (b + 1) * 128]
        prs[seq] = pblk[y]
        ex_o.start()

    def dec4():
        ex_o.wait()
        r = hid_ref[:, pl.ds(pl.multiple_of(y * 128, 128), 128)].astype(F32)
        for t in range(SEQ):
            r = r + prs[t]
        rmsg[...] = r
        rall[y] = r
        ex_r.start()

    def dec5():
        ex_r.wait()
        r = jnp.concatenate([rall[b] for b in range(4)], 1)
        squares = jnp.sum(r * r, axis=1, keepdims=True)
        x = (r * gain_ref[...].astype(F32)).astype(BF16)
        eye = iota((REQS, 128), 0) == iota((REQS, 128), 1)
        row = jnp.sum(jnp.where(eye, squares, 0.0), axis=0, keepdims=True)
        weight_wait(1)
        weight_wait(2)
        gate = jnp.dot(x, gwb[...], preferred_element_type=F32)
        upper = jnp.dot(x, uwb[...], preferred_element_type=F32)
        for t in range(GRP):
            gmsg[t, 0:32] = gate[:, t * 128 : (t + 1) * 128]
            gmsg[t, 32:64] = upper[:, t * 128 : (t + 1) * 128]
            gmsg[t, 64:72] = jnp.broadcast_to(row, (8, 128))
        grs[group] = gmsg[group]
        ex_g.start()

    def dec6():
        ex_g.wait()
        acc = grs[0]
        for t in range(1, GRP):
            acc = acc + grs[t]
        squares = as_column(acc[64:65, :], REQS)
        r = lax.rsqrt(squares / D + 1e-05)
        gate = acc[0:32] * r
        upper = acc[32:64] * r
        out = (gate / (1.0 + jnp.exp(-gate)) * upper).astype(BF16)
        hmsg[...] = out
        hall[group] = out
        ex_h.start()

    def dec7():
        ex_h.wait()
        hidden = jnp.concatenate([hall[t] for t in range(GRP)], 1)
        weight_wait(3)
        out = jnp.dot(hidden, dwb[...], preferred_element_type=F32)
        for b in range(4):
            dblk[b] = out[:, b * 128 : (b + 1) * 128]
        drs[seq] = dblk[y]
        ex_d.start()

    def dec8():
        ex_d.wait()
        out = rmsg[...]
        for t in range(SEQ):
            out = out + drs[t]
        dec_ref[...] = jnp.where(z == 0, out[:, 0:64], out[:, 64:128]).astype(BF16)

    steps = [dec0, dec1, dec2, dec3, dec4, dec5, dec6, dec7, dec8]

    def turn_body(it, carry):
        @pl.when(it < KVH)
        def _():
            relay_first(it)

        for i, dec in enumerate(steps):
            pl.when(it == i)(dec)

        @pl.when((it >= 1) & (it <= KVH))
        def _():
            relay_second(it - 1)

        @pl.when(it >= 2)
        def _():
            relay_third(it - 2)

        return carry

    lax.fori_loop(0, KVH + 2, turn_body, 0)

    def drain(h, carry):
        relay_last(h)
        relay_sent(h)
        return carry

    lax.fori_loop(0, KVH, drain, 0)


def step(meta, k, v, qn, kn, vn, hid, gain, ow, gw, uw, dw):
    vmem = pl.BlockSpec(memory_space=pltpu.VMEM)
    hbm = pl.BlockSpec(memory_space=pl.ANY)
    dma = pltpu.SemaphoreType.DMA
    return pl.pallas_call(
        step_kernel,
        out_shape=(
            jax.ShapeDtypeStruct((SEQ, KVH, 2, ROWS, HD), BF16),
            jax.ShapeDtypeStruct((REQS, 64), BF16),
        ),
        in_specs=[vmem] * 8 + [hbm] * 4,
        out_specs=(hbm, vmem),
        scratch_shapes=[
            pltpu.VMEM((1024, 512), BF16),
            pltpu.VMEM((512, 2048), BF16),
            pltpu.VMEM((512, 2048), BF16),
            pltpu.VMEM((2048, 512), BF16),
            pltpu.VMEM((32, 128), BF16),
            pltpu.VMEM((8, 32, 128), BF16),
            pltpu.VMEM((8, 2, 32, 128), F32),
            pltpu.VMEM((8, 2, 32, 128), F32),
            pltpu.VMEM((32, 128), BF16),
            pltpu.VMEM((16, 32, 128), BF16),
            pltpu.VMEM((4, 32, 128), F32),
            pltpu.VMEM((8, 32, 128), F32),
            pltpu.VMEM((32, 128), F32),
            pltpu.VMEM((4, 32, 128), F32),
            pltpu.VMEM((16, 72, 128), F32),
            pltpu.VMEM((16, 72, 128), F32),
            pltpu.VMEM((32, 128), BF16),
            pltpu.VMEM((16, 32, 128), BF16),
            pltpu.VMEM((4, 32, 128), F32),
            pltpu.VMEM((8, 32, 128), F32),
            dma((4,)),
            dma((8, 2)),
            dma((8, 7)),
            dma((8, 8)),
        ]
        + [dma((8,))] * 4
        + [dma((16,))] * 2
        + [dma((8,))] * 2
        + [dma((4,))] * 2
        + [dma((16,))] * 4
        + [dma((8,))] * 2,
        compiler_params=pltpu.CompilerParams(collective_id=0, has_side_effects=True, vmem_limit_bytes=40 << 20),
        name="step",
    )(meta, k, v, qn, kn, vn, hid, gain, ow, gw, uw, dw)


def shards(
    lengths, group_of, query_pre, key_pre, value_pre, query_new, key_new, value_new,
    hidden_new, out_weight, norm_gain, gate_weight, up_weight, down_weight,
):
    meta = jnp.pad(jnp.stack([lengths, group_of + 1]), ((0, 6), (0, 128 - REQS))) - jnp.array(
        [[0], [1], [0], [0], [0], [0], [0], [0]], jnp.int32
    )
    kvg, decode_hidden = step(
        meta, key_pre, value_pre, query_new, key_new, value_new, hidden_new, norm_gain.reshape(1, -1),
        out_weight, gate_weight, up_weight, down_weight,
    )
    return attend(meta, query_pre, kvg), decode_hidden


def solution(mesh):
    both = P(("grp", "seq"), None)
    return jax.shard_map(
        shards,
        mesh=mesh,
        in_specs=(
            P(), P(), both, both, both, P(None, "seq"), P(None, "seq"), P(None, "seq"), P(None, "grp"),
            P("seq", "grp"), P("grp"), P("grp", "seq"), P("grp", "seq"), P("seq", "grp"),
        ),
        out_specs=(both, P(None, ("grp", "seq"))),
        check_vma=False,
    )
```

time: 830 us -> 164 us (0.20)
  the two profiles are of different devices: /device:TPU:1 before, /device:TPU:88 now
where the time goes in v1:
time: 164 us; the launch traced here: 163 us
  Pallas kernels  148 us (90%)
  local copies, waits for them, and re-layouts  12.3 us (8%)
  other arithmetic  2.05 us (1%)
    pallas_call x1, Pallas kernels, step(): pl.pallas_call(step_kernel, out_shape=(jax.ShapeDtypeStruct((SEQ, KVH, 2,...  80.7 us
    pallas_call x1, Pallas kernels, attend(): pl.pallas_call(attend_kernel, grid=(KVH,), out_shape=jax.ShapeDtypeStruct...  67.3 us
    unnamed x21, local copies, waits for them, and re-layouts  11.7 us

profile of v1, /device:TPU:88, one launch (start us, length us, event | category | flops | bytes accessed | tf_op | source)
XLA Modules:
  0.0 163.1 jit_solution(1461315141761181403)
XLA Ops:
  0.6 0.7 add_bitcast_fusion
  1.3 0.7 pad_add_fusion.1
  2.0 0.7 reshape.7.gain_ref
  2.6 0.7 pad_add_fusion.meta_ref
  3.4 0.0 copy-start
  3.4 1.6 copy-done
  4.9 0.0 copy-start.1
  5.0 1.6 copy-done.1
  6.5 0.0 copy-start.2
  6.5 1.6 copy-done.2
  8.1 0.0 copy-start.3
  8.1 1.2 copy-done.3
  9.4 0.0 copy-start.4
  9.4 1.0 copy-done.4
  10.4 0.0 copy-start.5
  10.4 1.0 copy-done.5
  11.4 0.0 copy-start.6
  11.4 0.8 copy-done.6
  12.3 0.8 copy-done.7
  13.0 0.7 copy-done.8
  13.7 0.7 copy-done.9
  14.4 80.7 %step.1 = (bf16[8,8,2,256,128]{4,3,2,1,0:T(8,128)(2,1)}, bf16[32,64]{1,0:T(8,128)(2,1)S(1)}) custom-call(s32[8,128]{1,0:T(8,128)S(1)} %pad_add_fusion.meta_ref, bf16[256,1024]{1,0:T(8,128)(2,1)S(1)} %copy-done.4, bf16[256,1024]{1,0:T(8,128)(2,1)S(1)} %copy-done.5, bf16[32,1024]{1,0:T(8,128)(2,1)S(1)} %copy-done.6, bf16[32,128]{1,0:T(8,128)(2,1)S(1)} %copy-done.8, ...), custom_call_target="tpu_custom_call" | custom-call | tf_op jit(solution)/shard_map/step/pallas_call | solution.py:461
  95.2 67.3 %attend.1 = bf16[256,8192]{1,0:T(8,128)(2,1)} custom-call(s32[8,128]{1,0:T(8,128)S(1)} %pad_add_fusion.meta_ref, bf16[256,8192]{1,0:T(8,128)(2,1)} %q_ref.1, bf16[8,8,2,256,128]{4,3,2,1,0:T(8,128)(2,1)} %get-tuple-element.4.kv_ref), custom_call_target="tpu_custom_call" | custom-call | flops 18253611008 | bytes 16777216 | tf_op jit(solution)/shard_map/attend/pallas_call | solution.py:132
  162.5 0.6 copy.18
  (3 shorter events, 0.0 us)
Async XLA Ops:
  3.4 1.6 copy-start
  4.9 1.6 copy-start.1
  6.5 1.6 copy-start.2
  8.1 1.2 copy-start.3
  9.4 1.0 copy-start.4
  10.4 1.0 copy-start.5
  11.4 0.8 copy-start.6
  12.3 0.8 copy-start.7
  13.0 0.7 copy-start.8
  13.7 0.7 copy-start.9

commit v2 on v1

v2 whole, which is shorter than its diff:
```python
import functools
import math

import jax
import jax.numpy as jnp
from jax import lax
from jax.experimental import pallas as pl
from jax.experimental.pallas import tpu as pltpu
from jax.sharding import PartitionSpec as P

HD = 128
SEQ = 8
GRP = 16
ROWS = 256
KVH = 8
GROUPED = 8
REQS = 32
D = 8192
SCALE = 1.0 / math.sqrt(HD)
LOG2E = math.log2(math.e)
NEGATIVE = -1e30
FAR = -float(2**23)
F32 = jnp.float32
BF16 = jnp.bfloat16
NT = (((1,), (1,)), ((), ()))


def iota(shape, dim):
    return lax.broadcasted_iota(jnp.int32, shape, dim)


def as_column(row, count):
    eye = iota((count, 128), 0) == iota((count, 128), 1)
    return jnp.sum(jnp.where(eye, row, 0), axis=1, keepdims=True)


def request_tables(len_ref, grp_ref):
    lengths = jnp.concatenate([len_ref[...], jnp.zeros((1, 128 - REQS), jnp.int32)], 1)
    groups = jnp.concatenate([grp_ref[...], jnp.full((1, 128 - REQS), -1, jnp.int32)], 1)
    len_col = as_column(lengths, 128)
    grp_col = as_column(groups, 128)
    before = (grp_col == groups) & (iota((128, 128), 0) < iota((128, 128), 1))
    starts = jnp.sum(jnp.where(before, len_col, 0), axis=0, keepdims=True)
    ranks = jnp.sum(jnp.where(before, 1, 0), axis=0, keepdims=True)
    return lengths, groups, starts, ranks


def owner_onehot(tables, group, first, count):
    lengths, groups, starts, _ = tables
    slot = first + iota((count, 128), 0)
    return (groups == group) & (slot >= starts) & (slot < starts + lengths)


def remote(src, dst, send_sem, recv_sem, device):
    return pltpu.make_async_remote_copy(src_ref=src, dst_ref=dst, send_sem=send_sem, recv_sem=recv_sem, device_id=device)


class Exchange:
    def __init__(self, axis, count, me, source, landing, send_sem, recv_sem, spread=lambda i: i):
        self.axis, self.count, self.me, self.spread = axis, count, me, spread
        self.source, self.landing, self.send_sem, self.recv_sem = source, landing, send_sem, recv_sem

    def start(self):
        for i in range(1, self.count):
            peer = (self.me + i) % self.count
            remote(
                self.source(peer),
                self.landing.at[self.me],
                self.send_sem.at[i],
                self.recv_sem.at[self.me],
                {self.axis: self.spread(peer)},
            ).start()

    def wait(self):
        for i in range(1, self.count):
            peer = (self.me + i) % self.count
            copy = remote(
                self.source(peer),
                self.landing.at[peer],
                self.send_sem.at[i],
                self.recv_sem.at[peer],
                {self.axis: self.spread(peer)},
            )
            copy.wait_send()
            copy.wait_recv()


def step_kernel(
    len_hbm, grp_hbm, qn_hbm, kn_hbm, vn_hbm, hid_hbm, gain_hbm, ow_ref, gw_ref, uw_ref, dw_ref, q_ref, k_ref, v_ref,
    out_ref, dec_ref,
    len_ref, grp_ref, qn_ref, kn_ref, vn_ref, hid_ref, gain_ref,
    kvg, qb, ob, qx, kx, live, top, total, accum,
    owb, gwb, uwb, dwb, qmsg, qall, pmsg, part, amsg, aall, pblk, prs, rmsg, rall, gmsg, grs, hmsg, hall, dblk, drs,
    isem, wsem, lsem, qsem, osem, kss, krs, qss, qrs, pss, prsem, ass, ars, oss, ors, rss, rrs, gss, grsem, hss, hrs, dss, drsem,
):
    seq = lax.axis_index("seq")
    group = lax.axis_index("grp")
    y, z = seq // 2, seq % 2
    pair = seq + 1 - 2 * z
    up, down = (seq + 2) % SEQ, (seq + 6) % SEQ

    barrier = pltpu.get_barrier_semaphore()
    for i in range(1, SEQ):
        pl.semaphore_signal(barrier, inc=1, device_id={"seq": (seq + i) % SEQ})
    for i in range(1, GRP):
        pl.semaphore_signal(barrier, inc=1, device_id={"grp": (group + i) % GRP})

    def own_copy(h, which):
        src = (k_ref, v_ref)[which].at[:, pl.ds(pl.multiple_of(h * HD, HD), HD)]
        return pltpu.make_async_copy(src, kvg.at[seq, h, which], lsem.at[h, which])

    def own_start(h, carry):
        own_copy(h, 0).start()
        own_copy(h, 1).start()
        return carry

    small = [
        (len_hbm, len_ref), (grp_hbm, grp_ref), (qn_hbm, qn_ref), (kn_hbm, kn_ref),
        (vn_hbm, vn_ref), (hid_hbm, hid_ref), (gain_hbm, gain_ref),
    ]
    for i, (src, dst) in enumerate(small):
        pltpu.make_async_copy(src, dst, isem.at[i]).start()
    lax.fori_loop(0, KVH, own_start, 0)

    def q_copy(h):
        cols = pl.ds(pl.multiple_of(h * 1024, 1024), 1024)
        return pltpu.make_async_copy(q_ref.at[:, cols], qb.at[:, cols], qsem.at[h])

    def out_copy(h):
        cols = pl.ds(pl.multiple_of(h * 1024, 1024), 1024)
        return pltpu.make_async_copy(ob.at[h % 2], out_ref.at[:, cols], osem.at[h % 2])

    weights = [(ow_ref, owb), (gw_ref, gwb), (uw_ref, uwb), (dw_ref, dwb)]
    for i, (src, dst) in enumerate(weights):
        pltpu.make_async_copy(src, dst, wsem.at[i]).start()

    def weight_wait(i):
        pltpu.make_async_copy(weights[i][0], weights[i][1], wsem.at[i]).wait()

    def q_start(h, carry):
        q_copy(h).start()
        return carry

    lax.fori_loop(0, KVH, q_start, 0)
    for i, (src, dst) in enumerate(small):
        pltpu.make_async_copy(src, dst, isem.at[i]).wait()

    tables = request_tables(len_ref, grp_ref)
    lengths, groups, starts, ranks = tables
    slot32 = iota((REQS, 128), 0) % 4
    pick = (groups == group) & (ranks == slot32)
    pick32 = jnp.where(pick, 1.0, 0.0).astype(BF16)[:, 0:REQS]
    block32 = iota((REQS, HD), 0) // 4
    spread_q = jnp.dot(pick32, qn_ref[...], preferred_element_type=F32)
    mine_q = jnp.zeros((REQS, HD), F32)
    for a in range(GROUPED):
        mine_q = mine_q + jnp.where(block32 == a, spread_q[:, a * HD : (a + 1) * HD], 0.0)
    qmsg[...] = mine_q.astype(BF16)
    qall[seq] = mine_q.astype(BF16)

    lane = iota((ROWS, 128), 1)
    rows_in = owner_onehot(tables, group, seq * ROWS, ROWS)
    qx[...] = jnp.where(((lane < REQS) & jnp.logical_not(rows_in)) | (lane == 127), FAR, 0.0).astype(BF16)
    held = jnp.sum(jnp.where(rows_in, 1.0, 0.0), axis=1, keepdims=True)
    live[...] = jnp.broadcast_to(held, (ROWS, 128))
    for t in range(SEQ):
        cols_in = owner_onehot(tables, group, t * ROWS, ROWS)
        none = jnp.sum(jnp.where(cols_in, 1.0, 0.0), axis=1, keepdims=True) == 0.0
        kx[t * ROWS : (t + 1) * ROWS, :] = jnp.where(cols_in | (none & (lane == 127)), 1.0, 0.0).astype(BF16)

    def own_wait(h, carry):
        own_copy(h, 0).wait()
        own_copy(h, 1).wait()
        return carry

    lax.fori_loop(0, KVH, own_wait, 0)
    pl.semaphore_wait(barrier, SEQ + GRP - 2)

    ex_q = Exchange("seq", SEQ, seq, lambda p: qmsg, qall, qss, qrs)
    ex_p = Exchange("seq", SEQ, seq, lambda p: pmsg.at[p], part, pss, prsem)
    ex_a = Exchange("grp", GRP, group, lambda p: amsg, aall, ass, ars)
    ex_o = Exchange("seq", SEQ, seq, lambda p: pblk.at[p // 2], prs, oss, ors)
    ex_r = Exchange("seq", 4, y, lambda p: rmsg, rall, rss, rrs, lambda p: 2 * p + z)
    ex_g = Exchange("grp", GRP, group, lambda p: gmsg.at[p], grs, gss, grsem)
    ex_h = Exchange("grp", GRP, group, lambda p: hmsg, hall, hss, hrs)
    ex_d = Exchange("seq", SEQ, seq, lambda p: dblk.at[p // 2], drs, dss, drsem)

    def relay(h, slot, shard, dst):
        return remote(kvg.at[shard, h], kvg.at[shard, h], kss.at[h, slot], krs.at[shard, h], {"seq": dst})

    turn = ((y + 1) // 2 + 1) % 2
    cross = 2 * (1 - y % 2) + z
    far = (seq + 4) % SEQ

    def sends(h):
        return [
            (0, seq, pair, y >= 0),
            (1, seq, up, y < 3),
            (2, seq, down, (y == 0) | ((y == 1) & (h % 2 == 1))),
            (3, pair, up, y < 3),
            (4, pair, down, y == 0),
            (5, cross, (seq + 2 + 4 * turn) % SEQ, h % 2 == turn),
            (6, far, pair, y >= 2),
        ]

    def start(h, slots):
        for slot, shard, dst, on in sends(h):
            if slot in slots:

                @pl.when(on)
                def _():
                    relay(h, slot, shard, dst).start()

    def arrived(h, shard):
        relay(h, 0, shard, pair).wait_recv()

    def relay_first(h):
        start(h, (0, 1, 2))

    def relay_second(h):
        arrived(h, pair)
        start(h, (3, 4))

        @pl.when(h % 2 == turn)
        def _():
            arrived(h, cross)

        start(h, (5,))

    def relay_third(h):
        @pl.when(y >= 2)
        def _():
            arrived(h, far)

        start(h, (6,))

    def relay_last(h):
        for t in range(SEQ):
            seen = ((t == cross) & (h % 2 == turn)) | ((t == far) & (y >= 2))

            @pl.when((t // 2 < y) & jnp.logical_not(seen))
            def _():
                arrived(h, t)

    def relay_sent(h):
        for slot, shard, dst, on in sends(h):

            @pl.when(on)
            def _():
                relay(h, slot, shard, dst).wait_send()

    def dec0():
        ex_q.start()

    def dec1():
        ex_q.wait()
        start_c = jnp.sum(jnp.where(pick, starts, 0), axis=1, keepdims=True)
        len_c = jnp.sum(jnp.where(pick, lengths, 0), axis=1, keepdims=True)
        pos = seq * ROWS + iota((REQS, ROWS), 1)
        allowed = (pos >= start_c) & (pos < start_c + len_c)
        for t in range(SEQ):
            s = lax.dot_general(qall[t], kvg[seq, t, 0], NT, preferred_element_type=F32) * SCALE
            s = jnp.where(allowed, s, NEGATIVE)
            m = jnp.max(s, axis=1, keepdims=True)
            p = jnp.where(allowed, jnp.exp(s - m), 0.0)
            l = jnp.sum(p, axis=1, keepdims=True)
            pmsg[t, 0] = jnp.dot(p.astype(BF16), kvg[seq, t, 1], preferred_element_type=F32)
            pmsg[t, 1] = jnp.where(iota((REQS, HD), 1) == 0, m, l)
        part[seq] = pmsg[seq]
        ex_p.start()

    def dec2():
        ex_p.wait()
        key_row = jnp.dot(pick32, kn_ref[...], preferred_element_type=F32)
        value_row = jnp.dot(pick32, vn_ref[...], preferred_element_type=F32)
        own = jnp.sum(qmsg[...].astype(F32) * key_row, axis=1, keepdims=True) * SCALE
        top = own
        for t in range(SEQ):
            top = jnp.maximum(top, part[t, 1][:, 0:1])
        weight = jnp.exp(own - top)
        total = weight
        mixed = weight.astype(BF16).astype(F32) * value_row
        for t in range(SEQ):
            scale = jnp.exp(part[t, 1][:, 0:1] - top)
            total = total + scale * part[t, 1][:, 1:2]
            mixed = mixed + scale * part[t, 0]
        out = (mixed / total).astype(BF16)
        amsg[...] = out
        aall[group] = out
        ex_a.start()

    def dec3():
        ex_a.wait()
        rank_col = as_column(ranks, REQS)
        grp_col = as_column(groups, REQS)
        target = jnp.concatenate([grp_col * 32 + a * 4 + rank_col for a in range(GROUPED)], 0)
        gather = jnp.where(iota((256, 512), 1) == target, 1.0, 0.0).astype(BF16)
        rows = jnp.dot(gather, aall[...].reshape(512, HD), preferred_element_type=F32).astype(BF16)
        att = jnp.concatenate([rows[a * 32 : (a + 1) * 32] for a in range(GROUPED)], 1)
        weight_wait(0)
        proj = jnp.dot(att, owb[...], preferred_element_type=F32)
        for b in range(4):
            pblk[b] = proj[:, b * 128 : (b + 1) * 128]
        prs[seq] = pblk[y]
        ex_o.start()

    def dec4():
        ex_o.wait()
        r = hid_ref[:, pl.ds(pl.multiple_of(y * 128, 128), 128)].astype(F32)
        for t in range(SEQ):
            r = r + prs[t]
        rmsg[...] = r
        rall[y] = r
        ex_r.start()

    def dec5():
        ex_r.wait()
        r = jnp.concatenate([rall[b] for b in range(4)], 1)
        squares = jnp.sum(r * r, axis=1, keepdims=True)
        x = (r * gain_ref[...].astype(F32)).astype(BF16)
        eye = iota((REQS, 128), 0) == iota((REQS, 128), 1)
        row = jnp.sum(jnp.where(eye, squares, 0.0), axis=0, keepdims=True)
        weight_wait(1)
        weight_wait(2)
        gate = jnp.dot(x, gwb[...], preferred_element_type=F32)
        upper = jnp.dot(x, uwb[...], preferred_element_type=F32)
        for t in range(GRP):
            gmsg[t, 0:32] = gate[:, t * 128 : (t + 1) * 128]
            gmsg[t, 32:64] = upper[:, t * 128 : (t + 1) * 128]
            gmsg[t, 64:72] = jnp.broadcast_to(row, (8, 128))
        grs[group] = gmsg[group]
        ex_g.start()

    def dec6():
        ex_g.wait()
        acc = grs[0]
        for t in range(1, GRP):
            acc = acc + grs[t]
        squares = as_column(acc[64:65, :], REQS)
        r = lax.rsqrt(squares / D + 1e-05)
        gate = acc[0:32] * r
        upper = acc[32:64] * r
        out = (gate / (1.0 + jnp.exp(-gate)) * upper).astype(BF16)
        hmsg[...] = out
        hall[group] = out
        ex_h.start()

    def dec7():
        ex_h.wait()
        hidden = jnp.concatenate([hall[t] for t in range(GRP)], 1)
        weight_wait(3)
        out = jnp.dot(hidden, dwb[...], preferred_element_type=F32)
        for b in range(4):
            dblk[b] = out[:, b * 128 : (b + 1) * 128]
        drs[seq] = dblk[y]
        ex_d.start()

    def dec8():
        ex_d.wait()
        out = rmsg[...]
        for t in range(SEQ):
            out = out + drs[t]
        dec_ref[...] = jnp.where(z == 0, out[:, 0:64], out[:, 64:128]).astype(BF16)

    steps = [dec0, dec1, dec2, dec3, dec4, dec5, dec6, dec7, dec8]

    def block(h, j, diagonal):
        keys = kvg[pl.ds(2 * j, 2), h, 0].reshape(512, HD)
        values = kvg[pl.ds(2 * j, 2), h, 1].reshape(512, HD)
        keys = jnp.concatenate([keys, kx[pl.ds(pl.multiple_of(j * 512, 512), 512), :]], 1)
        if diagonal:
            causal = (j * 512 + iota((ROWS, 512), 1)) <= (seq * ROWS + iota((ROWS, 512), 0))
        scores = []
        for a in range(GROUPED):
            cols = pl.ds(pl.multiple_of((h * GROUPED + a) * HD, HD), HD)
            queries = jnp.concatenate([qb[:, cols], qx[...]], 1)
            scores.append(lax.dot_general(queries, keys, NT, preferred_element_type=F32))
        for a in range(GROUPED):
            s = scores[a]
            if diagonal:
                s = jnp.where(causal, s, NEGATIVE)
            old = top[a]
            m = s[:, 0:128]
            for i in range(1, 4):
                m = jnp.maximum(m, s[:, i * 128 : (i + 1) * 128])
            new = jnp.maximum(old, jnp.max(m, axis=1, keepdims=True))
            decay = jnp.exp2((old - new) * (SCALE * LOG2E))
            shift = new * (SCALE * LOG2E)
            p = jnp.concatenate(
                [jnp.exp2(s[:, i * 128 : (i + 1) * 128] * (SCALE * LOG2E) - shift) for i in range(4)], 1
            )
            t = p[:, 0:128]
            for i in range(1, 4):
                t = t + p[:, i * 128 : (i + 1) * 128]
            total[a] = total[a] * decay + t
            top[a] = new
            accum[a] = accum[a] * decay + jnp.dot(p.astype(BF16), values, preferred_element_type=F32)

    def attend(h):
        q_copy(h).wait()
        top[...] = jnp.full((GROUPED, ROWS, 128), NEGATIVE, F32)
        total[...] = jnp.zeros((GROUPED, ROWS, 128), F32)
        accum[...] = jnp.zeros((GROUPED, ROWS, 128), F32)

        def each(j, carry):
            block(h, j, False)
            return carry

        lax.fori_loop(0, y, each, 0)
        block(h, y, True)

        @pl.when(h >= 2)
        def _():
            out_copy(h).wait()

        for a in range(GROUPED):
            t = jnp.sum(total[a], axis=1, keepdims=True)
            ok = live[...] > 0.0
            ob[h % 2, :, a * HD : (a + 1) * HD] = jnp.where(ok, accum[a] / t, 0.0).astype(BF16)
        out_copy(h).start()

    def turn_body(it, carry):
        @pl.when((it >= 1) & (it <= KVH))
        def _():
            relay_second(it - 1)

        @pl.when((it >= 2) & (it <= KVH + 1))
        def _():
            relay_third(it - 2)

        @pl.when(it < KVH)
        def _():
            relay_first(it)

        for i, dec in enumerate(steps):
            pl.when(it == i)(dec)

        @pl.when(it >= 3)
        def _():
            relay_last(it - 3)
            attend(it - 3)

        return carry

    lax.fori_loop(0, KVH + 3, turn_body, 0)

    def drain(h, carry):
        relay_sent(h)
        return carry

    lax.fori_loop(0, KVH, drain, 0)
    out_copy(KVH - 2).wait()
    out_copy(KVH - 1).wait()


def step(*operands):
    vmem = pl.BlockSpec(memory_space=pltpu.VMEM)
    hbm = pl.BlockSpec(memory_space=pl.ANY)
    dma = pltpu.SemaphoreType.DMA
    return pl.pallas_call(
        step_kernel,
        out_shape=(
            jax.ShapeDtypeStruct((ROWS, D), BF16),
            jax.ShapeDtypeStruct((REQS, 64), BF16),
        ),
        in_specs=[hbm] * 14,
        out_specs=(hbm, vmem),
        scratch_shapes=[
            pltpu.VMEM((1, 32), jnp.int32),
            pltpu.VMEM((1, 32), jnp.int32),
            pltpu.VMEM((32, 1024), BF16),
            pltpu.VMEM((32, 128), BF16),
            pltpu.VMEM((32, 128), BF16),
            pltpu.VMEM((32, 512), BF16),
            pltpu.VMEM((1, 512), BF16),
            pltpu.VMEM((SEQ, KVH, 2, ROWS, HD), BF16),
            pltpu.VMEM((ROWS, D), BF16),
            pltpu.VMEM((2, ROWS, 1024), BF16),
            pltpu.VMEM((ROWS, 128), BF16),
            pltpu.VMEM((SEQ * ROWS, 128), BF16),
            pltpu.VMEM((ROWS, 128), F32),
            pltpu.VMEM((GROUPED, ROWS, 128), F32),
            pltpu.VMEM((GROUPED, ROWS, 128), F32),
            pltpu.VMEM((GROUPED, ROWS, 128), F32),
            pltpu.VMEM((1024, 512), BF16),
            pltpu.VMEM((512, 2048), BF16),
            pltpu.VMEM((512, 2048), BF16),
            pltpu.VMEM((2048, 512), BF16),
            pltpu.VMEM((32, 128), BF16),
            pltpu.VMEM((8, 32, 128), BF16),
            pltpu.VMEM((8, 2, 32, 128), F32),
            pltpu.VMEM((8, 2, 32, 128), F32),
            pltpu.VMEM((32, 128), BF16),
            pltpu.VMEM((16, 32, 128), BF16),
            pltpu.VMEM((4, 32, 128), F32),
            pltpu.VMEM((8, 32, 128), F32),
            pltpu.VMEM((32, 128), F32),
            pltpu.VMEM((4, 32, 128), F32),
            pltpu.VMEM((16, 72, 128), F32),
            pltpu.VMEM((16, 72, 128), F32),
            pltpu.VMEM((32, 128), BF16),
            pltpu.VMEM((16, 32, 128), BF16),
            pltpu.VMEM((4, 32, 128), F32),
            pltpu.VMEM((8, 32, 128), F32),
            dma((7,)),
            dma((4,)),
            dma((8, 2)),
            dma((8,)),
            dma((2,)),
            dma((8, 7)),
            dma((8, 8)),
        ]
        + [dma((8,))] * 4
        + [dma((16,))] * 2
        + [dma((8,))] * 2
        + [dma((4,))] * 2
        + [dma((16,))] * 4
        + [dma((8,))] * 2,
        compiler_params=pltpu.CompilerParams(collective_id=0, has_side_effects=True, vmem_limit_bytes=58 << 20),
        name="step",
    )(*operands)


def shards(
    lengths, group_of, query_pre, key_pre, value_pre, query_new, key_new, value_new,
    hidden_new, out_weight, norm_gain, gate_weight, up_weight, down_weight,
):
    return step(
        lengths.reshape(1, -1), group_of.reshape(1, -1), query_new, key_new, value_new, hidden_new,
        norm_gain.reshape(1, -1), out_weight, gate_weight, up_weight, down_weight, query_pre, key_pre, value_pre,
    )


def solution(mesh):
    both = P(("grp", "seq"), None)
    return jax.shard_map(
        shards,
        mesh=mesh,
        in_specs=(
            P(), P(), both, both, both, P(None, "seq"), P(None, "seq"), P(None, "seq"), P(None, "grp"),
            P("seq", "grp"), P("grp"), P("grp", "seq"), P("grp", "seq"), P("seq", "grp"),
        ),
        out_specs=(both, P(None, ("grp", "seq"))),
        check_vma=False,
    )
```

time: 164 us -> 115 us (0.70)
  the two profiles are of different devices: /device:TPU:88 before, /device:TPU:56 now
where the time goes in v2:
time: 115 us; the launch traced here: 114 us
  Pallas kernels  107 us (93%)
  local copies, waits for them, and re-layouts  6.51 us (6%)
    pallas_call x1, Pallas kernels, step(): pl.pallas_call(step_kernel, out_shape=(jax.ShapeDtypeStruct((ROWS, D), BF...  107 us
    unnamed x4, local copies, waits for them, and re-layouts  5.25 us

profile of v2, /device:TPU:56, one launch (start us, length us, event | category | flops | bytes accessed | tf_op | source)
XLA Modules:
  0.0 114.2 jit_solution(356928404455149224)
XLA Ops:
  0.6 1.3 %reshape.15.gain_hbm = bf16[1,512]{1,0:T(2,128)(2,1)} reshape(bf16[512]{0:T(512)(128)(2,1)} %param.24) | data formatting | bytes 2048 | tf_op jit(solution)/shard_map/reshape | solution.py:530
  1.9 107.1 %step.1 = (bf16[256,8192]{1,0:T(8,128)(2,1)}, bf16[32,64]{1,0:T(8,128)(2,1)}) custom-call(s32[1,32]{1,0:T(1,128)} %bitcast.2, s32[1,32]{1,0:T(1,128)} %bitcast.3, bf16[32,1024]{1,0:T(8,128)(2,1)} %qn_hbm.1, bf16[32,128]{1,0:T(8,128)(2,1)} %kn_hbm.1, bf16[32,128]{1,0:T(8,128)(2,1)} %vn_hbm.1, bf16[32,512]{1,0:T(8,128)(2,1)} %hid_hbm.1, ...), custom_call_target="tpu_custom_call" | custom-call | tf_op jit(solution)/shard_map/step/pallas_call | solution.py:460
  109.0 0.0 copy-start
  109.0 4.6 %copy.18 = bf16[256,8192]{1,0:T(8,128)(2,1)} copy(bf16[256,8192]{1,0:T(8,128)(2,1)} %get-tuple-element.4) | data formatting | bytes 8388608
  113.6 0.0 copy-done
  113.6 0.6 copy.19
Async XLA Ops:
  109.0 4.7 %copy-start = (bf16[32,64]{1,0:T(8,128)(2,1)S(1)}, bf16[32,64]{1,0:T(8,128)(2,1)}, u32[]{:S(2)}) copy-start(bf16[32,64]{1,0:T(8,128)(2,1)} %get-tuple-element.5) | copy-start | bytes 12292

commit v3 on v2

--- a/solution.py
+++ b/solution.py
@@ -13,6 +13,7 @@
 GRP = 16
 ROWS = 256
 KVH = 8
+LAG = 5
 GROUPED = 8
 REQS = 32
 D = 8192
@@ -214,20 +215,23 @@
     def arrived(h, shard):
         relay(h, 0, shard, pair).wait_recv()
 
-    def relay_first(h):
-        start(h, (0, 1, 2))
-
-    def relay_second(h):
-        arrived(h, pair)
+    def relay_pair(h):
+        start(h, (0,))
+
+    def relay_own(h):
+        start(h, (1, 2))
+
+    def relay_other(h):
         start(h, (3, 4))
 
+    def relay_cross(h):
         @pl.when(h % 2 == turn)
         def _():
             arrived(h, cross)
 
         start(h, (5,))
 
-    def relay_third(h):
+    def relay_far(h):
         @pl.when(y >= 2)
         def _():
             arrived(h, far)
@@ -364,85 +368,131 @@
 
     steps = [dec0, dec1, dec2, dec3, dec4, dec5, dec6, dec7, dec8]
 
-    def block(h, j, diagonal):
+    def products(h, j):
         keys = kvg[pl.ds(2 * j, 2), h, 0].reshape(512, HD)
-        values = kvg[pl.ds(2 * j, 2), h, 1].reshape(512, HD)
         keys = jnp.concatenate([keys, kx[pl.ds(pl.multiple_of(j * 512, 512), 512), :]], 1)
-        if diagonal:
-            causal = (j * 512 + iota((ROWS, 512), 1)) <= (seq * ROWS + iota((ROWS, 512), 0))
         scores = []
         for a in range(GROUPED):
             cols = pl.ds(pl.multiple_of((h * GROUPED + a) * HD, HD), HD)
             queries = jnp.concatenate([qb[:, cols], qx[...]], 1)
             scores.append(lax.dot_general(queries, keys, NT, preferred_element_type=F32))
+        return scores
+
+    def folded(parts, op):
+        return functools.reduce(op, [parts[:, i * 128 : (i + 1) * 128] for i in range(4)])
+
+    def weigh(s, new):
+        shift = new * (SCALE * LOG2E)
+        return jnp.concatenate(
+            [jnp.exp2(s[:, i * 128 : (i + 1) * 128] * (SCALE * LOG2E) - shift) for i in range(4)], 1
+        )
+
+    def diagonal(h):
+        arrived(h, pair)
+        q_copy(h).wait()
+        values = kvg[pl.ds(2 * y, 2), h, 1].reshape(512, HD)
+        causal = (y * 512 + iota((ROWS, 512), 1)) <= (seq * ROWS + iota((ROWS, 512), 0))
+        scores = products(h, y)
+        for a in range(GROUPED):
+            s = jnp.where(causal, scores[a], NEGATIVE)
+            new = jnp.max(folded(s, jnp.maximum), axis=1, keepdims=True)
+            new = jnp.broadcast_to(new, (ROWS, 128))
+            p = weigh(s, new)
+            total[h, a] = folded(p, jnp.add)
+            top[h, a] = new
+            accum[h, a] = jnp.dot(p.astype(BF16), values, preferred_element_type=F32)
+
+    def block(h, j):
+        values = kvg[pl.ds(2 * j, 2), h, 1].reshape(512, HD)
+        scores = products(h, j)
         for a in range(GROUPED):
             s = scores[a]
-            if diagonal:
-                s = jnp.where(causal, s, NEGATIVE)
-            old = top[a]
-            m = s[:, 0:128]
-            for i in range(1, 4):
-                m = jnp.maximum(m, s[:, i * 128 : (i + 1) * 128])
-            new = jnp.maximum(old, jnp.max(m, axis=1, keepdims=True))
+            old = top[h, a]
+            new = jnp.maximum(old, jnp.max(folded(s, jnp.maximum), axis=1, keepdims=True))
             decay = jnp.exp2((old - new) * (SCALE * LOG2E))
-            shift = new * (SCALE * LOG2E)
-            p = jnp.concatenate(
-                [jnp.exp2(s[:, i * 128 : (i + 1) * 128] * (SCALE * LOG2E) - shift) for i in range(4)], 1
-            )
-            t = p[:, 0:128]
-            for i in range(1, 4):
-                t = t + p[:, i * 128 : (i + 1) * 128]
-            total[a] = total[a] * decay + t
-            top[a] = new
-            accum[a] = accum[a] * decay + jnp.dot(p.astype(BF16), values, preferred_element_type=F32)
-
-    def attend(h):
-        q_copy(h).wait()
-        top[...] = jnp.full((GROUPED, ROWS, 128), NEGATIVE, F32)
-        total[...] = jnp.zeros((GROUPED, ROWS, 128), F32)
-        accum[...] = jnp.zeros((GROUPED, ROWS, 128), F32)
-
+            p = weigh(s, new)
+            total[h, a] = total[h, a] * decay + folded(p, jnp.add)
+            top[h, a] = new
+            accum[h, a] = accum[h, a] * decay + jnp.dot(p.astype(BF16), values, preferred_element_type=F32)
+
+    def when_head(h, action):
+        @pl.when(h < KVH)
+        def _():
+            action(h)
+
+    def middle(h):
+        when_head(h + 1, relay_far)
+        when_head(h + 6, relay_pair)
+        when_head(h + 3, relay_cross)
+        when_head(h + 3, relay_other)
+        when_head(h + 5, relay_own)
+
+    def rest(h):
         def each(j, carry):
-            block(h, j, False)
+            @pl.when(j == y // 2)
+            def _():
+                middle(h)
+
+            block(h, j)
             return carry
 
         lax.fori_loop(0, y, each, 0)
-        block(h, y, True)
+
+        @pl.when(y == 0)
+        def _():
+            middle(h)
 
         @pl.when(h >= 2)
         def _():
             out_copy(h).wait()
 
         for a in range(GROUPED):
-            t = jnp.sum(total[a], axis=1, keepdims=True)
+            t = jnp.sum(total[h, a], axis=1, keepdims=True)
             ok = live[...] > 0.0
-            ob[h % 2, :, a * HD : (a + 1) * HD] = jnp.where(ok, accum[a] / t, 0.0).astype(BF16)
+            ob[h % 2, :, a * HD : (a + 1) * HD] = jnp.where(ok, accum[h, a] / t, 0.0).astype(BF16)
         out_copy(h).start()
 
-    def turn_body(it, carry):
-        @pl.when((it >= 1) & (it <= KVH))
-        def _():
-            relay_second(it - 1)
-
-        @pl.when((it >= 2) & (it <= KVH + 1))
-        def _():
-            relay_third(it - 2)
-
-        @pl.when(it < KVH)
-        def _():
-            relay_first(it)
-
-        for i, dec in enumerate(steps):
-            pl.when(it == i)(dec)
-
-        @pl.when(it >= 3)
-        def _():
-            relay_last(it - 3)
-            attend(it - 3)
+    relay_pair(0)
+    relay_own(0)
+    dec0()
+    relay_pair(1)
+    relay_own(1)
+    relay_pair(2)
+    relay_pair(3)
+    opening = {
+        0: [(relay_cross, 0), (relay_other, 0), (relay_own, 2), (dec1, None)],
+        1: [(relay_far, 0), (relay_pair, 4)],
+        2: [(relay_cross, 1), (relay_other, 1), (relay_own, 3)],
+        3: [(relay_pair, 5), (dec2, None)],
+        4: [(relay_cross, 2), (relay_other, 2), (relay_own, 4)],
+    }
+
+    def open_head(i, carry):
+        diagonal(i)
+        for k, actions in opening.items():
+
+            @pl.when(i == k)
+            def _():
+                for action, head in actions:
+                    action() if head is None else action(head)
 
         return carry
 
-    lax.fori_loop(0, KVH + 3, turn_body, 0)
+    def turn_body(i, carry):
+        @pl.when(i >= LAG)
+        def _():
+            relay_last(i - LAG)
+            rest(i - LAG)
+
+        @pl.when(i < KVH)
+        def _():
+            open_head(i, 0)
+
+        for k, dec in enumerate(steps[3:]):
+            pl.when(i == LAG + k)(dec)
+        return carry
+
+    lax.fori_loop(0, KVH + LAG, turn_body, 0)
 
     def drain(h, carry):
         relay_sent(h)
@@ -479,9 +529,9 @@
             pltpu.VMEM((ROWS, 128), BF16),
             pltpu.VMEM((SEQ * ROWS, 128), BF16),
             pltpu.VMEM((ROWS, 128), F32),
-            pltpu.VMEM((GROUPED, ROWS, 128), F32),
-            pltpu.VMEM((GROUPED, ROWS, 128), F32),
-            pltpu.VMEM((GROUPED, ROWS, 128), F32),
+            pltpu.VMEM((KVH, GROUPED, ROWS, 128), F32),
+            pltpu.VMEM((KVH, GROUPED, ROWS, 128), F32),
+            pltpu.VMEM((KVH, GROUPED, ROWS, 128), F32),
             pltpu.VMEM((1024, 512), BF16),
             pltpu.VMEM((512, 2048), BF16),
             pltpu.VMEM((512, 2048), BF16),

time: 115 us -> 105 us (0.913)
  Pallas kernels: 107 us -> 96.7 us
    pallas_call x1, Pallas kernels: 107 us -> 96.7 us  [step(): pl.pallas_call(step_kernel, out_shape=(jax.ShapeDtypeStruct((ROWS, D), BF...]
where the time goes in v3:
time: 105 us; the launch traced here: 104 us
  Pallas kernels  96.7 us (92%)
  local copies, waits for them, and re-layouts  6.51 us (6%)
    pallas_call x1, Pallas kernels, step(): pl.pallas_call(step_kernel, out_shape=(jax.ShapeDtypeStruct((ROWS, D), BF...  96.7 us
    unnamed x4, local copies, waits for them, and re-layouts  5.25 us

profile of v3, /device:TPU:56, one launch (start us, length us, event | category | flops | bytes accessed | tf_op | source)
XLA Modules:
  0.0 103.9 jit_solution(18340620915629782594)
XLA Ops:
  0.6 1.3 %reshape.15.gain_hbm = bf16[1,512]{1,0:T(2,128)(2,1)} reshape(bf16[512]{0:T(512)(128)(2,1)} %param.24) | data formatting | bytes 2048 | tf_op jit(solution)/shard_map/reshape | solution.py:580
  1.9 96.7 %step.1 = (bf16[256,8192]{1,0:T(8,128)(2,1)}, bf16[32,64]{1,0:T(8,128)(2,1)}) custom-call(s32[1,32]{1,0:T(1,128)} %bitcast.2, s32[1,32]{1,0:T(1,128)} %bitcast.3, bf16[32,1024]{1,0:T(8,128)(2,1)} %qn_hbm.1, bf16[32,128]{1,0:T(8,128)(2,1)} %kn_hbm.1, bf16[32,128]{1,0:T(8,128)(2,1)} %vn_hbm.1, bf16[32,512]{1,0:T(8,128)(2,1)} %hid_hbm.1, ...), custom_call_target="tpu_custom_call" | custom-call | tf_op jit(solution)/shard_map/step/pallas_call | solution.py:510
  98.6 0.0 copy-start
  98.6 4.6 %copy.18 = bf16[256,8192]{1,0:T(8,128)(2,1)} copy(bf16[256,8192]{1,0:T(8,128)(2,1)} %get-tuple-element.4) | data formatting | bytes 8388608
  103.3 0.0 copy-done
  103.3 0.6 copy.19
Async XLA Ops:
  98.6 4.7 %copy-start = (bf16[32,64]{1,0:T(8,128)(2,1)S(1)}, bf16[32,64]{1,0:T(8,128)(2,1)}, u32[]{:S(2)}) copy-start(bf16[32,64]{1,0:T(8,128)(2,1)} %get-tuple-element.5) | copy-start | bytes 12292

commit v4 on v3

--- a/solution.py
+++ b/solution.py
@@ -13,7 +13,6 @@
 GRP = 16
 ROWS = 256
 KVH = 8
-LAG = 5
 GROUPED = 8
 REQS = 32
 D = 8192
@@ -36,8 +35,8 @@
 
 
 def request_tables(len_ref, grp_ref):
-    lengths = jnp.concatenate([len_ref[...], jnp.zeros((1, 128 - REQS), jnp.int32)], 1)
-    groups = jnp.concatenate([grp_ref[...], jnp.full((1, 128 - REQS), -1, jnp.int32)], 1)
+    lengths = jnp.concatenate([len_ref[...].reshape(1, -1), jnp.zeros((1, 128 - REQS), jnp.int32)], 1)
+    groups = jnp.concatenate([grp_ref[...].reshape(1, -1), jnp.full((1, 128 - REQS), -1, jnp.int32)], 1)
     len_col = as_column(lengths, 128)
     grp_col = as_column(groups, 128)
     before = (grp_col == groups) & (iota((128, 128), 0) < iota((128, 128), 1))
@@ -222,6 +221,7 @@
         start(h, (1, 2))
 
     def relay_other(h):
+        arrived(h, pair)
         start(h, (3, 4))
 
     def relay_cross(h):
@@ -321,7 +321,7 @@
         ex_r.wait()
         r = jnp.concatenate([rall[b] for b in range(4)], 1)
         squares = jnp.sum(r * r, axis=1, keepdims=True)
-        x = (r * gain_ref[...].astype(F32)).astype(BF16)
+        x = (r * gain_ref[...].astype(F32).reshape(1, -1)).astype(BF16)
         eye = iota((REQS, 128), 0) == iota((REQS, 128), 1)
         row = jnp.sum(jnp.where(eye, squares, 0.0), axis=0, keepdims=True)
         weight_wait(1)
@@ -368,9 +368,9 @@
 
     steps = [dec0, dec1, dec2, dec3, dec4, dec5, dec6, dec7, dec8]
 
-    def products(h, j):
-        keys = kvg[pl.ds(2 * j, 2), h, 0].reshape(512, HD)
-        keys = jnp.concatenate([keys, kx[pl.ds(pl.multiple_of(j * 512, 512), 512), :]], 1)
+    def products(h, keys, first):
+        count = keys.shape[0]
+        keys = jnp.concatenate([keys, kx[pl.ds(pl.multiple_of(first * ROWS, ROWS), count), :]], 1)
         scores = []
         for a in range(GROUPED):
             cols = pl.ds(pl.multiple_of((h * GROUPED + a) * HD, HD), HD)
@@ -379,20 +379,19 @@
         return scores
 
     def folded(parts, op):
-        return functools.reduce(op, [parts[:, i * 128 : (i + 1) * 128] for i in range(4)])
+        return functools.reduce(op, [parts[:, i : i + 128] for i in range(0, parts.shape[1], 128)])
 
     def weigh(s, new):
         shift = new * (SCALE * LOG2E)
         return jnp.concatenate(
-            [jnp.exp2(s[:, i * 128 : (i + 1) * 128] * (SCALE * LOG2E) - shift) for i in range(4)], 1
+            [jnp.exp2(s[:, i : i + 128] * (SCALE * LOG2E) - shift) for i in range(0, s.shape[1], 128)], 1
         )
 
     def diagonal(h):
-        arrived(h, pair)
         q_copy(h).wait()
-        values = kvg[pl.ds(2 * y, 2), h, 1].reshape(512, HD)
-        causal = (y * 512 + iota((ROWS, 512), 1)) <= (seq * ROWS + iota((ROWS, 512), 0))
-        scores = products(h, y)
+        values = kvg[seq, h, 1]
+        causal = iota((ROWS, ROWS), 1) <= iota((ROWS, ROWS), 0)
+        scores = products(h, kvg[seq, h, 0], seq)
         for a in range(GROUPED):
             s = jnp.where(causal, scores[a], NEGATIVE)
             new = jnp.max(folded(s, jnp.maximum), axis=1, keepdims=True)
@@ -402,9 +401,8 @@
             top[h, a] = new
             accum[h, a] = jnp.dot(p.astype(BF16), values, preferred_element_type=F32)
 
-    def block(h, j):
-        values = kvg[pl.ds(2 * j, 2), h, 1].reshape(512, HD)
-        scores = products(h, j)
+    def block(h, keys, values, first):
+        scores = products(h, keys, first)
         for a in range(GROUPED):
             s = scores[a]
             old = top[h, a]
@@ -422,10 +420,10 @@
 
     def middle(h):
         when_head(h + 1, relay_far)
-        when_head(h + 6, relay_pair)
-        when_head(h + 3, relay_cross)
-        when_head(h + 3, relay_other)
-        when_head(h + 5, relay_own)
+        when_head(h + 2, relay_cross)
+        when_head(h + 2, relay_other)
+        when_head(h + 4, relay_own)
+        when_head(h + 5, relay_pair)
 
     def rest(h):
         def each(j, carry):
@@ -433,8 +431,14 @@
             def _():
                 middle(h)
 
-            block(h, j)
+            keys = kvg[pl.ds(2 * j, 2), h, 0].reshape(512, HD)
+            values = kvg[pl.ds(2 * j, 2), h, 1].reshape(512, HD)
+            block(h, keys, values, 2 * j)
             return carry
+
+        @pl.when(z == 1)
+        def _():
+            block(h, kvg[pair, h, 0], kvg[pair, h, 1], pair)
 
         lax.fori_loop(0, y, each, 0)
 
@@ -457,14 +461,12 @@
     dec0()
     relay_pair(1)
     relay_own(1)
-    relay_pair(2)
-    relay_pair(3)
     opening = {
-        0: [(relay_cross, 0), (relay_other, 0), (relay_own, 2), (dec1, None)],
-        1: [(relay_far, 0), (relay_pair, 4)],
-        2: [(relay_cross, 1), (relay_other, 1), (relay_own, 3)],
-        3: [(relay_pair, 5), (dec2, None)],
-        4: [(relay_cross, 2), (relay_other, 2), (relay_own, 4)],
+        2: [(relay_cross, 0), (relay_other, 0), (relay_own, 2), (relay_pair, 2)],
+        3: [(dec1, None)],
+        5: [(relay_far, 0), (relay_pair, 3)],
+        6: [(relay_cross, 1), (relay_other, 1), (relay_own, 3), (relay_pair, 4)],
+        7: [(dec2, None)],
     }
 
     def open_head(i, carry):
@@ -478,21 +480,16 @@
 
         return carry
 
-    def turn_body(i, carry):
-        @pl.when(i >= LAG)
-        def _():
-            relay_last(i - LAG)
-            rest(i - LAG)
-
-        @pl.when(i < KVH)
-        def _():
-            open_head(i, 0)
-
+    lax.fori_loop(0, KVH, open_head, 0)
+
+    def close_head(h, carry):
+        relay_last(h)
+        rest(h)
         for k, dec in enumerate(steps[3:]):
-            pl.when(i == LAG + k)(dec)
+            pl.when(h == k)(dec)
         return carry
 
-    lax.fori_loop(0, KVH + LAG, turn_body, 0)
+    lax.fori_loop(0, KVH, close_head, 0)
 
     def drain(h, carry):
         relay_sent(h)
@@ -516,13 +513,13 @@
         in_specs=[hbm] * 14,
         out_specs=(hbm, vmem),
         scratch_shapes=[
-            pltpu.VMEM((1, 32), jnp.int32),
-            pltpu.VMEM((1, 32), jnp.int32),
+            pltpu.VMEM((32,), jnp.int32),
+            pltpu.VMEM((32,), jnp.int32),
             pltpu.VMEM((32, 1024), BF16),
             pltpu.VMEM((32, 128), BF16),
             pltpu.VMEM((32, 128), BF16),
             pltpu.VMEM((32, 512), BF16),
-            pltpu.VMEM((1, 512), BF16),
+            pltpu.VMEM((512,), BF16),
             pltpu.VMEM((SEQ, KVH, 2, ROWS, HD), BF16),
             pltpu.VMEM((ROWS, D), BF16),
             pltpu.VMEM((2, ROWS, 1024), BF16),
@@ -576,8 +573,8 @@
     hidden_new, out_weight, norm_gain, gate_weight, up_weight, down_weight,
 ):
     return step(
-        lengths.reshape(1, -1), group_of.reshape(1, -1), query_new, key_new, value_new, hidden_new,
-        norm_gain.reshape(1, -1), out_weight, gate_weight, up_weight, down_weight, query_pre, key_pre, value_pre,
+        lengths, group_of, query_new, key_new, value_new, hidden_new,
+        norm_gain, out_weight, gate_weight, up_weight, down_weight, query_pre, key_pre, value_pre,
     )
 
 

time: 105 us -> 98.3 us (0.936)
  Pallas kernels: 96.7 us -> 92.3 us
  local copies, waits for them, and re-layouts: 6.51 us -> 5.25 us
    pallas_call x1, Pallas kernels: 96.7 us -> 92.3 us  [step(): pl.pallas_call(step_kernel, out_shape=(jax.ShapeDtypeStruct((ROWS, D), BF...]
    reshape x1 -> x0, local copies, waits for them, and re-layouts: 1.26 us -> none  [shards(): norm_gain.reshape(1, -1)]
where the time goes in v4:
time: 98.3 us; the launch traced here: 98.2 us
  Pallas kernels  92.3 us (94%)
  local copies, waits for them, and re-layouts  5.25 us (5%)
    pallas_call x1, Pallas kernels, step(): pl.pallas_call(step_kernel, out_shape=(jax.ShapeDtypeStruct((ROWS, D), BF...  92.3 us
    unnamed x4, local copies, waits for them, and re-layouts  5.25 us

profile of v4, /device:TPU:56, one launch (start us, length us, event | category | flops | bytes accessed | tf_op | source)
XLA Modules:
  0.0 98.2 jit_solution(3285306015909764092)
XLA Ops:
  0.6 92.3 %step.1 = (bf16[256,8192]{1,0:T(8,128)(2,1)}, bf16[32,64]{1,0:T(8,128)(2,1)}) custom-call(s32[32]{0:T(128)} %len_hbm.1, s32[32]{0:T(128)} %grp_hbm.1, bf16[32,1024]{1,0:T(8,128)(2,1)} %qn_hbm.1, bf16[32,128]{1,0:T(8,128)(2,1)} %kn_hbm.1, bf16[32,128]{1,0:T(8,128)(2,1)} %vn_hbm.1, bf16[32,512]{1,0:T(8,128)(2,1)} %hid_hbm.1, bf16[512]{0:T(512)(128)(2,1)} %gain_hbm.1, ...), custom_call_target="tpu_custom_call" | custom-call | tf_op jit(solution)/shard_map/step/pallas_call | solution.py:507
  92.9 0.0 copy-start
  93.0 4.6 %copy.18 = bf16[256,8192]{1,0:T(8,128)(2,1)} copy(bf16[256,8192]{1,0:T(8,128)(2,1)} %get-tuple-element.4) | data formatting | bytes 8388608
  97.6 0.0 copy-done
  97.6 0.6 copy.19
Async XLA Ops:
  92.9 4.7 %copy-start = (bf16[32,64]{1,0:T(8,128)(2,1)S(1)}, bf16[32,64]{1,0:T(8,128)(2,1)}, u32[]{:S(2)}) copy-start(bf16[32,64]{1,0:T(8,128)(2,1)} %get-tuple-element.5) | copy-start | bytes 12292

commit v5 on v4

--- a/solution.py
+++ b/solution.py
@@ -568,14 +568,52 @@
     )(*operands)
 
 
+def hand_over_kernel(att_ref, dec_ref, att_out, dec_out, att_buf, dec_buf, read_sems, write_sems):
+    reads = [pltpu.make_async_copy(dec_ref, dec_buf, read_sems.at[8])]
+    writes = [pltpu.make_async_copy(dec_buf, dec_out, write_sems.at[8])]
+    for i in range(8):
+        rows = pl.ds(i * 32, 32)
+        reads.append(pltpu.make_async_copy(att_ref.at[rows], att_buf.at[rows], read_sems.at[i]))
+        writes.append(pltpu.make_async_copy(att_buf.at[rows], att_out.at[rows], write_sems.at[i]))
+    for read in reads:
+        read.start()
+    for read, write in zip(reads, writes):
+        read.wait()
+        write.start()
+    for write in writes:
+        write.wait()
+
+
+def hand_over(attention, decode_hidden):
+    hbm = pl.BlockSpec(memory_space=pl.ANY)
+    return pl.pallas_call(
+        hand_over_kernel,
+        out_shape=(
+            jax.ShapeDtypeStruct(attention.shape, BF16),
+            jax.ShapeDtypeStruct(decode_hidden.shape, BF16),
+        ),
+        in_specs=[hbm] * 2,
+        out_specs=(hbm, hbm),
+        scratch_shapes=[
+            pltpu.VMEM(attention.shape, BF16),
+            pltpu.VMEM(decode_hidden.shape, BF16),
+            pltpu.SemaphoreType.DMA((9,)),
+            pltpu.SemaphoreType.DMA((9,)),
+        ],
+        compiler_params=pltpu.CompilerParams(vmem_limit_bytes=60 << 20),
+        name="hand_over",
+    )(attention, decode_hidden)
+
+
 def shards(
     lengths, group_of, query_pre, key_pre, value_pre, query_new, key_new, value_new,
     hidden_new, out_weight, norm_gain, gate_weight, up_weight, down_weight,
 ):
-    return step(
+    attention, decode_hidden = step(
         lengths, group_of, query_new, key_new, value_new, hidden_new,
         norm_gain, out_weight, gate_weight, up_weight, down_weight, query_pre, key_pre, value_pre,
     )
+    return hand_over(attention, decode_hidden)
 
 
 def solution(mesh):

time: 98.3 us -> 96.8 us (0.985)
  local copies, waits for them, and re-layouts: 5.25 us -> 0 us
  Pallas kernels: 92.3 us -> 96 us
    unnamed x4 -> x0, local copies, waits for them, and re-layouts: 5.25 us -> none
    pallas_call x0 -> x1, Pallas kernels: none -> 3.64 us  [hand_over(): pl.pallas_call(hand_over_kernel, out_shape=(jax.ShapeDtypeStruct(attentio...]
where the time goes in v5:
time: 96.8 us; the launch traced here: 96.6 us
  Pallas kernels  96 us (99%)
    pallas_call x1, Pallas kernels, step(): pl.pallas_call(step_kernel, out_shape=(jax.ShapeDtypeStruct((ROWS, D), BF...  92.3 us
    pallas_call x1, Pallas kernels, hand_over(): pl.pallas_call(hand_over_kernel, out_shape=(jax.ShapeDtypeStruct(attentio...  3.64 us

profile of v5, /device:TPU:56, one launch (start us, length us, event | category | flops | bytes accessed | tf_op | source)
XLA Modules:
  0.0 96.6 jit_solution(2120494790226712230)
XLA Ops:
  0.6 92.3 %step.1 = (bf16[256,8192]{1,0:T(8,128)(2,1)}, bf16[32,64]{1,0:T(8,128)(2,1)}) custom-call(s32[32]{0:T(128)} %len_hbm.1, s32[32]{0:T(128)} %grp_hbm.1, bf16[32,1024]{1,0:T(8,128)(2,1)} %qn_hbm.1, bf16[32,128]{1,0:T(8,128)(2,1)} %kn_hbm.1, bf16[32,128]{1,0:T(8,128)(2,1)} %vn_hbm.1, bf16[32,512]{1,0:T(8,128)(2,1)} %hid_hbm.1, bf16[512]{0:T(512)(128)(2,1)} %gain_hbm.1, ...), custom_call_target="tpu_custom_call" | custom-call | tf_op jit(solution)/shard_map/step/pallas_call | solution.py:507
  93.0 3.6 %hand_over.1 = (bf16[256,8192]{1,0:T(8,128)(2,1)}, bf16[32,64]{1,0:T(8,128)(2,1)}) custom-call(bf16[256,8192]{1,0:T(8,128)(2,1)} %get-tuple-element.4.att_ref, bf16[32,64]{1,0:T(8,128)(2,1)} %get-tuple-element.5.dec_ref), custom_call_target="tpu_custom_call" | custom-call | tf_op jit(solution)/shard_map/hand_over/pallas_call | solution.py:589
